TPU v7x, 32 devices: a whole 2x2x4 slice. The times are simulated.
32 devices in a mesh: depth: 4 (over y, core), lat: 8 (over z, x).
Axes of the slice: x: 2, y: 2, z: 4, core: 2. Of those that a mesh axis runs over, the one named last changes fastest.
Arguments:
- fields: float32 [4, 2, 2, 2, 512, 512], P('depth', None, None, None, 'lat'), may hold values from -6 to 6
- surface: float32 [2, 2, 2, 512, 512], P(None, None, None, 'lat'), may hold values from -6 to 6
- held_freqs: int32 [4, 2], P('depth'), may hold values from 8 to 63
- surface_freqs: int32 [2], replicated, may hold values from 8 to 63
- ref_slowness: float32 [4, 1, 2], P('depth'), may hold values from 0.6 to 1.2
- weights: float32 [4, 1, 512, 512], P('depth', None, 'lat'), may hold values from 0 to 1
- regions: int32 [4, 1, 512, 512], P('depth', None, 'lat'), may hold values from 0 to 7
- region_slowness: float32 [4, 1, 8], P('depth'), may hold values from 0.6 to 1.2
Outputs:
- fields_out: float32 [4, 2, 2, 2, 512, 512], P('depth', None, None, None, 'lat')
- image_out: float32 [4, 1, 16, 512, 512], P('depth', None, None, 'lat')
All inputs are finite; a program needn't handle non-finite values.
Results may differ from a plain program's by a relative error of at most 0.0003.
Values sent between devices are 32-bit elements; how exact they have to be, the bound alone decides.
A program may use at most 64 MiB of HBM per device.

v0:
```python
import functools
import math

import jax
import jax.numpy as jnp
import ml_dtypes
import numpy as np
from jax import lax
from jax.experimental import pallas as pl
from jax.experimental.pallas import tpu as pltpu
from jax.sharding import PartitionSpec as P

LAGS = 16
REGIONS = 8


omega_step = 0.04
depth_step = 1.0
exact_math = lax.Precision.HIGHEST


def with_halo(cells, sides, width):
    for axis, dim in sides:
        count = lax.axis_size(axis)
        ends = count - 1
        head = lax.slice_in_dim(cells, 0, width, axis=dim)
        tail = lax.slice_in_dim(cells, cells.shape[dim] - width, cells.shape[dim], axis=dim)
        cells = jnp.concatenate(
            [
                lax.ppermute(tail, axis, [(i, (i + 1) % count) for i in range(ends)]),
                cells,
                lax.ppermute(head, axis, [((i + 1) % count, i) for i in range(ends)]),
            ],
            axis=dim,
        )
    return cells


def passed_along(value, axis, steps):
    count = lax.axis_size(axis)
    leading, last = (max(0, -steps), min(count, count - steps))
    return lax.ppermute(value, axis, [(source, source + steps) for source in range(leading, last)])


def factor_pair(length):
    first_len = 1
    for divisor in range(1, math.isqrt(length) + 1):
        if length % divisor == 0:
            first_len = divisor
    return (first_len, length // first_len)


def unit_phase(product_index, period, direction):
    turning = direction * 2.0 * math.pi / period * product_index.astype(jnp.float32)
    return (jnp.cos(turning), jnp.sin(turning))


def transform_tables(first_len, second_len, direction):
    first_range = jnp.arange(first_len, dtype=jnp.int32)
    second_range = jnp.arange(second_len, dtype=jnp.int32)
    outer_table = unit_phase(
        first_range[:, None] * first_range[None, :] % first_len, first_len, direction
    )
    twist_table = unit_phase(
        first_range[:, None] * second_range[None, :] % (first_len * second_len),
        first_len * second_len,
        direction,
    )
    inner_table = unit_phase(
        second_range[:, None] * second_range[None, :] % second_len, second_len, direction
    )
    return (outer_table, twist_table, inner_table)


def complex_product(pattern, values, table_pair):
    real_times = jnp.einsum(pattern, values[0], table_pair[0], precision=exact_math)
    imag_times = jnp.einsum(pattern, values[1], table_pair[1], precision=exact_math)
    joint_times = jnp.einsum(
        pattern, values[0] + values[1], table_pair[0] + table_pair[1], precision=exact_math
    )
    return jnp.stack([real_times - imag_times, joint_times - real_times - imag_times])


def complex_scale(values, factor):
    return jnp.stack(
        [
            values[0] * factor[0] - values[1] * factor[1],
            values[0] * factor[1] + values[1] * factor[0],
        ]
    )


def wave_numbers(positions, length):
    folded = jnp.where(positions < length // 2, positions, positions - length)
    return folded.astype(jnp.float32) * (2.0 * math.pi / length)


def forward_rows(values, tables, lane_count):
    groups, row_count, col_count = (values.shape[1], values.shape[2], values.shape[3])
    outer_table, twist_table, inner_table = tables
    split_first = outer_table[0].shape[0]
    split_second = inner_table[0].shape[0]
    shaped = values.reshape(2, groups, row_count, split_first, split_second)
    segmented = complex_product("grjm,kj->gkmr", shaped, outer_table)
    segmented = complex_scale(segmented, (twist_table[0][:, :, None], twist_table[1][:, :, None]))
    segmented = complex_product("gkmr,lm->gklr", segmented, inner_table)
    return segmented.reshape(2, groups, lane_count, col_count * row_count // lane_count)


def forward_columns(values, tables, lane_count, col_block, row_count):
    groups = values.shape[1]
    outer_table, twist_table, inner_table = tables
    shaped = values.reshape(2, groups, lane_count, col_block, row_count)
    segmented = complex_product("gscr,ks->gkcr", shaped, outer_table)
    segmented = complex_scale(segmented, (twist_table[0][:, None, :], twist_table[1][:, None, :]))
    segmented = complex_product("gkcr,lr->gckl", segmented, inner_table)
    return segmented.reshape(2, groups, col_block, lane_count * row_count)


def inverse_columns(values, tables, lane_count, row_count):
    groups, col_block = (values.shape[1], values.shape[2])
    outer_table, twist_table, inner_table = tables
    shaped = values.reshape(2, groups, col_block, lane_count, row_count)
    segmented = complex_product("gckl,lr->gckr", shaped, inner_table)
    segmented = complex_scale(segmented, twist_table)
    segmented = complex_product("gckr,ks->gscr", segmented, outer_table)
    return segmented.reshape(2, groups, lane_count, col_block * row_count)


def inverse_rows(values, tables, depth_rows):
    groups = values.shape[1]
    outer_table, twist_table, inner_table = tables
    split_first = outer_table[0].shape[0]
    split_second = inner_table[0].shape[0]
    shaped = values.reshape(2, groups, split_first, split_second, depth_rows)
    segmented = complex_product("gklr,lm->gkmr", shaped, inner_table)
    segmented = complex_scale(segmented, (twist_table[0][:, :, None], twist_table[1][:, :, None]))
    segmented = complex_product("gkmr,kj->grjm", segmented, outer_table)
    return segmented.reshape(2, groups, depth_rows, split_first * split_second)


def level_step(
    wave_state, omega_batch, slow_pair, weight_rows, cell_rows, squared, tables_y, tables_x, layout
):
    lane_count, row_count, col_block, margin = layout
    freq_count = wave_state.shape[2]
    col_count = wave_state.shape[4]
    sign_pair = jnp.array([-1.0, 1.0], jnp.float32)
    flat_state = wave_state.reshape(2, 2 * freq_count, row_count, col_count)
    spectra = forward_rows(flat_state, tables_y[0], lane_count)
    spectra = lax.all_to_all(spectra, "lat", split_axis=2, concat_axis=2, tiled=True)
    spectra = forward_columns(spectra, tables_x[0], lane_count, col_block, row_count)
    spectra = spectra.reshape(2, 2, freq_count, col_block, lane_count * row_count)
    wave_base = omega_batch[None, :, None, None] * slow_pair[:, None, None, None]
    wave_gap = wave_base * wave_base - squared[None, None]
    amplitude = jnp.exp(-jnp.sqrt(jnp.maximum(-wave_gap, 0.0)) * depth_step)
    turning = (
        sign_pair[None, :, None, None, None]
        * jnp.sqrt(jnp.maximum(wave_gap, 0.0))[:, None]
        * depth_step
    )
    factor = (amplitude[:, None] * jnp.cos(turning), amplitude[:, None] * jnp.sin(turning))
    shifted = complex_scale(spectra[:, None], factor)
    shifted = shifted.reshape(2, 4 * freq_count, col_block, lane_count * row_count)
    returned = inverse_columns(shifted, tables_x[1], lane_count, row_count)
    returned = lax.all_to_all(returned, "lat", split_axis=2, concat_axis=2, tiled=True)
    depth_rows = row_count + 2 * margin
    ref_fields = inverse_rows(returned, tables_y[1], depth_rows)
    ref_fields = ref_fields.reshape(2, 2, 2, freq_count, depth_rows, col_count) * (
        1.0 / (lane_count * row_count * col_count)
    )
    mixed_field = weight_rows * ref_fields[:, 0] + (1.0 - weight_rows) * ref_fields[:, 1]
    blend_slow = weight_rows * slow_pair[0] + (1.0 - weight_rows) * slow_pair[1]
    lens_angle = (
        sign_pair[:, None, None, None]
        * omega_batch[None, :, None, None]
        * (cell_rows - blend_slow)[None, None]
        * depth_step
    )
    return complex_scale(mixed_field, (jnp.cos(lens_angle), jnp.sin(lens_angle)))


def lag_products(padded, half_lags, row_count):
    lag_terms = []
    for lag_index in range(2 * half_lags):
        offset = lag_index - half_lags
        source_rows = padded[:, 0, :, half_lags - offset : half_lags - offset + row_count]
        receiver_rows = padded[:, 1, :, half_lags + offset : half_lags + offset + row_count]
        lag_terms.append(jnp.sum(source_rows * receiver_rows, axis=(0, 1)))
    return jnp.stack(lag_terms)


def shards(
    fields, surface, held_freqs, surface_freqs, ref_slowness, weights, regions, region_slowness
):
    lane_count = lax.axis_size("lat")
    row_count = fields.shape[4]
    col_count = fields.shape[5]
    col_block = col_count // lane_count
    total_rows = lane_count * row_count
    half_lags = LAGS // 2
    split_first, split_second = factor_pair(col_count)
    tables_y = (
        transform_tables(split_first, split_second, -1.0),
        transform_tables(split_first, split_second, 1.0),
    )
    tables_x = (
        transform_tables(lane_count, row_count, -1.0),
        transform_tables(lane_count, row_count, 1.0),
    )
    block_index = lax.axis_index("lat")
    storage_y = block_index * col_block + jnp.arange(col_block, dtype=jnp.int32)
    index_y = storage_y // split_second + split_first * (storage_y % split_second)
    storage_x = jnp.arange(total_rows, dtype=jnp.int32)
    index_x = storage_x // row_count + lane_count * (storage_x % row_count)
    squared = (
        wave_numbers(index_y, col_count)[:, None] ** 2
        + wave_numbers(index_x, total_rows)[None, :] ** 2
    )
    region_ids = jnp.arange(REGIONS, dtype=jnp.int32)
    matches = (regions[0][None] == region_ids[:, None, None, None]).astype(jnp.float32)
    cell_slowness = jnp.sum(matches * jnp.transpose(region_slowness[0])[:, :, None, None], axis=0)
    margin = 0
    weight_rows_all = weights[0]
    layout = (lane_count, row_count, col_block, margin)
    wave_state = fields[0]
    omega_batch = held_freqs[0].astype(jnp.float32) * omega_step
    images = [jnp.zeros((LAGS, row_count, col_count), jnp.float32)]
    for tick_index in range(2):
        result = level_step(
            wave_state,
            omega_batch,
            ref_slowness[0, 0],
            weight_rows_all[0],
            cell_slowness[0],
            squared,
            tables_y,
            tables_x,
            layout,
        )
        wave_state = result
        padded = with_halo(result, (("lat", 3),), half_lags)
        images[0] = images[0] + lag_products(padded, half_lags, row_count)
        if tick_index == 0:
            moved, moved_omega = passed_along((wave_state, omega_batch), "depth", 1)
            at_top = lax.axis_index("depth") == 0
            wave_state = jnp.where(at_top, surface, moved)
            omega_batch = jnp.where(
                at_top, surface_freqs.astype(jnp.float32) * omega_step, moved_omega
            )
    return (wave_state[None], jnp.stack(images)[None])

def split_halves(value):
    high = value.astype(jnp.bfloat16)
    low = (value - high.astype(jnp.float32)).astype(jnp.bfloat16)
    return (high, low)


def dft_tables(length):
    index = np.arange(length)
    turning = 2.0 * np.pi / length * (index[:, None] * index[None, :] % length)
    tables = []
    for exact in (np.cos(turning), np.sin(turning)):
        high = exact.astype(ml_dtypes.bfloat16)
        low = (exact - high.astype(np.float64)).astype(ml_dtypes.bfloat16)
        tables += [high, low]
    return np.stack(tables)


def dot(left, right):
    return jnp.dot(left, right, preferred_element_type=jnp.float32)


def three_pass_left(tables, which, high, low):
    table_high, table_low = (tables[2 * which], tables[2 * which + 1])
    return dot(table_high, high) + (dot(table_high, low) + dot(table_low, high))


def three_pass_right(tables, which, high, low):
    table_high, table_low = (tables[2 * which], tables[2 * which + 1])
    return dot(high, table_high) + (dot(low, table_high) + dot(high, table_low))


def dft_left(tables, values, direction):
    half = values.shape[1] // 2
    high, low = split_halves(values)
    even = three_pass_left(tables, 0, high, low)
    odd = three_pass_left(tables, 1, high, low)
    return (
        even[:, :half] - direction * odd[:, half:],
        even[:, half:] + direction * odd[:, :half],
    )


def dft_right(tables, values, direction):
    half = values.shape[0] // 2
    high, low = split_halves(values)
    even = three_pass_right(tables, 0, high, low)
    odd = three_pass_right(tables, 1, high, low)
    return (
        even[:half] - direction * odd[half:],
        even[half:] + direction * odd[:half],
    )


def spread_rows(core, tables, values, keep_ref, send_ref):
    half = values.shape[0] // 2
    real, imag = dft_left(tables, values, -1.0)
    both = jnp.concatenate([real, imag], axis=1)
    first, second = (both[:half], both[half:])
    at_first = core == 0
    keep_ref[...] = jnp.where(at_first, first, second)
    send_ref[...] = jnp.where(at_first, second, first)


def start_kernel(core_ref, blocks_ref, tables_ref, keep_ref, send_ref):
    spread_rows(core_ref[0], tables_ref, blocks_ref[...], keep_ref, send_ref)


def folded(positions, length):
    moved = jnp.where(positions < length // 2, positions, positions - length)
    return moved.astype(jnp.float32) * (2.0 * math.pi / length)


def middle_kernel(scale, core_ref, numbers_ref, own_ref, other_ref, tables_ref, keep_ref, send_ref):
    core = core_ref[0]
    at_first = core == 0
    rows, width = own_ref.shape
    half = width // 2
    own, other = (own_ref[...], other_ref[...])
    first = jnp.where(at_first, own, other)
    second = jnp.where(at_first, other, own)
    values = jnp.concatenate(
        [
            jnp.concatenate([first[:, :half], second[:, :half]], axis=1),
            jnp.concatenate([first[:, half:], second[:, half:]], axis=1),
        ],
        axis=0,
    )
    real, imag = dft_right(tables_ref, values, -1.0)
    kx = folded(lax.broadcasted_iota(jnp.int32, (rows, 1), 0) + core * rows, 2 * rows)
    ky = folded(lax.broadcasted_iota(jnp.int32, (1, width), 1), width)
    squared = kx * kx + ky * ky
    omega, sign = (numbers_ref[0], numbers_ref[1])
    for ref_index in range(2):
        base = omega * numbers_ref[2 + ref_index]
        gap = base * base - squared
        amplitude = jnp.exp(-jnp.sqrt(jnp.maximum(-gap, 0.0))) * scale
        turning = jnp.sqrt(jnp.maximum(gap, 0.0))
        cosine = amplitude * jnp.cos(turning)
        sine = amplitude * (sign * jnp.sin(turning))
        shifted = jnp.concatenate([real * cosine - imag * sine, real * sine + imag * cosine], axis=0)
        back_real, back_imag = dft_right(tables_ref, shifted, 1.0)
        first = jnp.concatenate([back_real[:, :half], back_imag[:, :half]], axis=1)
        second = jnp.concatenate([back_real[:, half:], back_imag[:, half:]], axis=1)
        keep_ref[ref_index] = jnp.where(at_first, first, second)
        send_ref[ref_index] = jnp.where(at_first, second, first)


def continued(core, numbers_ref, own_ref, other_ref, cells_ref, tables_ref):
    at_first = core == 0
    rows, width = own_ref.shape[1:]
    half = width // 2
    fields = []
    for ref_index in range(2):
        own, other = (own_ref[ref_index], other_ref[ref_index])
        values = jnp.concatenate(
            [jnp.where(at_first, own, other), jnp.where(at_first, other, own)], axis=0
        )
        fields.append(dft_left(tables_ref, values, 1.0))
    weight = cells_ref[:, 0].reshape(2 * rows, half)
    cell = cells_ref[:, 1].reshape(2 * rows, half)
    rest = 1.0 - weight
    real = weight * fields[0][0] + rest * fields[1][0]
    imag = weight * fields[0][1] + rest * fields[1][1]
    blend = weight * numbers_ref[2] + rest * numbers_ref[3]
    angle = numbers_ref[1] * numbers_ref[0] * (cell - blend)
    cosine, sine = (jnp.cos(angle), jnp.sin(angle))
    return jnp.concatenate([real * cosine - imag * sine, real * sine + imag * cosine], axis=1)


def put_blocks(values, blocks_ref):
    count, tall, width = blocks_ref.shape
    rows = values.shape[0] // count
    margin = (tall - rows) // 2
    edge = jnp.zeros((margin, width), jnp.float32)
    for block in range(count):
        start = block * rows
        blocks_ref[block, margin : margin + rows] = values[start : start + rows]
        blocks_ref[block, :margin] = values[start - margin : start] if block else edge
        after = start + rows
        blocks_ref[block, margin + rows :] = (
            values[after : after + margin] if block < count - 1 else edge
        )


def turn_kernel(
    core_ref,
    numbers_ref,
    own_ref,
    other_ref,
    cells_ref,
    surface_ref,
    tables_ref,
    blocks_ref,
    keep_ref,
    send_ref,
):
    result = continued(core_ref[0], numbers_ref, own_ref, other_ref, cells_ref, tables_ref)
    put_blocks(result, blocks_ref)
    values = jnp.where(core_ref[1] == 1, surface_ref[...], result)
    spread_rows(core_ref[0], tables_ref, values, keep_ref, send_ref)


def end_kernel(
    core_ref, numbers_ref, own_ref, other_ref, cells_ref, tables_ref, blocks_ref
):
    result = continued(core_ref[0], numbers_ref, own_ref, other_ref, cells_ref, tables_ref)
    put_blocks(result, blocks_ref)


def image_kernel(add, first_ref, second_ref, *refs):
    image_ref = refs[-1]
    lags, rows, width = image_ref.shape
    half = width // 2
    half_lags = lags // 2
    pairs = first_ref.shape[0] // 2
    for side, field_ref in enumerate((first_ref, second_ref)):
        for lag in range(lags):
            offset = lag - half_lags
            total = None
            for pair in range(pairs):
                source = field_ref[pair, half_lags - offset : half_lags - offset + rows, :]
                receiver = field_ref[
                    pairs + pair, half_lags + offset : half_lags + offset + rows, :
                ]
                term = source * receiver
                term = term[:, :half] + term[:, half:]
                total = term if total is None else total + term
            columns = slice(side * half, (side + 1) * half)
            if add:
                total = total + refs[0][lag, :, columns]
            image_ref[lag, :, columns] = total


def call(kernel, outs, *args):
    smem = {0, 1} if kernel_numbers(args) else {0}
    specs = [
        pl.BlockSpec(memory_space=pltpu.SMEM if place in smem else pltpu.VMEM)
        for place in range(len(args))
    ]
    return pl.pallas_call(
        kernel,
        out_shape=[jax.ShapeDtypeStruct(shape, jnp.float32) for shape in outs],
        in_specs=specs,
        out_specs=[pl.BlockSpec(memory_space=pltpu.VMEM)] * len(outs),
        compiler_params=pltpu.CompilerParams(vmem_limit_bytes=50 << 20),
    )(*args)


def kernel_numbers(args):
    return args[1].ndim == 1


def call_image(add, first, second, previous, shape):
    args = (first, second) + ((previous,) if add else ())
    return pl.pallas_call(
        functools.partial(image_kernel, add),
        out_shape=jax.ShapeDtypeStruct(shape, jnp.float32),
        in_specs=[pl.BlockSpec(memory_space=pltpu.VMEM)] * len(args),
        out_specs=pl.BlockSpec(memory_space=pltpu.VMEM),
        compiler_params=pltpu.CompilerParams(vmem_limit_bytes=50 << 20),
    )(*args)


def chip_shards(
    fields, surface, held_freqs, surface_freqs, ref_slowness, weights, regions, region_slowness
):
    lat = lax.axis_size("lat")
    depth = lax.axis_size("depth")
    depth_index = lax.axis_index("depth")
    core = depth_index % 2
    block_index = lax.axis_index("lat")
    place = block_index % 2
    field = block_index // 2
    at_first = core == 0
    freq_count = held_freqs.shape[1]
    field_count = 2 * freq_count
    rows, width = (fields.shape[4], fields.shape[5])
    half = width // 2
    total_rows = rows * lat
    half_lags = LAGS // 2
    swap = [(d, d + 1 - 2 * (d % 2)) for d in range(depth)]
    tables = jnp.asarray(dft_tables(width))

    def halves(value):
        first, second = (value[..., :half], value[..., half:])
        return (jnp.where(at_first, first, second), jnp.where(at_first, second, first))

    def swapped(value):
        return lax.ppermute(value, "depth", swap)

    def sent(blocks):
        return lax.all_to_all(blocks, "lat", split_axis=0, concat_axis=0, tiled=True)

    def side_by_side(value):
        return jnp.concatenate([value[0], value[1]], axis=-1)

    flat = fields[0].reshape(2, field_count, rows, width)
    own, other = halves(flat)
    own, other = (side_by_side(own), swapped(side_by_side(other)))
    both = jnp.stack(
        [jnp.where(at_first, own, other), jnp.where(at_first, other, own)], axis=1
    ).reshape(lat, rows, width)
    held = sent(both).reshape(total_rows, width)

    region_ids = jnp.arange(REGIONS, dtype=jnp.int32)
    cell = jnp.zeros((rows, width), jnp.float32)
    for region in range(REGIONS):
        cell = jnp.where(regions[0, 0] == region, region_slowness[0, 0, region], cell)
    numbers = jnp.concatenate(
        [ref_slowness[0, 0], held_freqs[0].astype(jnp.float32) * omega_step]
    )
    other_numbers = swapped(numbers)
    after_first = [((d + 2) % depth, d) for d in range(0, depth, 2)]
    after_second = [((d + 2) % depth, d + 1) for d in range(0, depth, 2)]

    def fetched(for_first, for_second):
        return jnp.where(
            at_first,
            lax.ppermute(for_first, "depth", after_first),
            lax.ppermute(for_second, "depth", after_second),
        )

    next_numbers = fetched(numbers, numbers)
    section_numbers = (
        jnp.where(at_first, numbers, other_numbers),
        jnp.where(at_first, other_numbers, numbers),
        next_numbers,
    )
    first_numbers = jnp.where(place == 0, section_numbers[0], section_numbers[1])
    second_numbers = jnp.where(place == 0, section_numbers[1], section_numbers[2])
    takes_surface = (depth_index // 2 == depth // 2 - 1) & (place == 1)
    freq = field % freq_count
    freq_ids = jnp.arange(freq_count, dtype=jnp.int32)

    def picked(values):
        return jnp.sum(jnp.where(freq_ids == freq, values, 0.0))

    sign = jnp.where(field < freq_count, -1.0, 1.0)
    omega_one = picked(first_numbers[2:])
    omega_two = jnp.where(
        takes_surface, picked(surface_freqs.astype(jnp.float32) * omega_step), omega_one
    )
    numbers_one = jnp.stack([omega_one, sign, first_numbers[0], first_numbers[1]])
    numbers_two = jnp.stack([omega_two, sign, second_numbers[0], second_numbers[1]])
    core_pair = jnp.stack([core, takes_surface.astype(jnp.int32)])

    cells = jnp.stack([weights[0, 0], cell])
    own_cells, other_cells = halves(cells)
    other_cells = swapped(other_cells)
    third = fetched(cells[..., :half], cells[..., half:])
    zero = jnp.where(at_first, own_cells, other_cells)
    one = jnp.where(at_first, other_cells, own_cells)

    def cell_blocks(even, odd):
        pair = jnp.stack([even, odd])
        return jnp.broadcast_to(pair[None], (lat // 2,) + pair.shape).reshape(
            (lat,) + even.shape
        )

    cells_one = sent(cell_blocks(zero, one))
    cells_two = sent(cell_blocks(one, third))
    surface_half, _ = halves(surface.reshape(2, field_count, rows, width))
    surface_half = side_by_side(surface_half)
    surface_blocks = jnp.broadcast_to(
        surface_half[:, None], (field_count, 2, rows, width)
    ).reshape(lat, rows, width)
    above = sent(surface_blocks).reshape(total_rows, width)

    spread = [(total_rows // 2, width)] * 2
    shifted = [(2, total_rows // 2, width)] * 2
    blocks = (lat, rows + 2 * half_lags, width)
    middle = functools.partial(middle_kernel, 1.0 / (total_rows * width))
    image_shape = (LAGS, rows, width)

    keep, send = call(start_kernel, spread, core_pair, held, tables)
    keep, send = call(middle, shifted, core_pair, numbers_one, keep, swapped(send), tables)
    result, keep, send = call(
        turn_kernel,
        [blocks] + spread,
        core_pair,
        numbers_one,
        keep,
        swapped(send),
        cells_one,
        above,
        tables,
    )
    first_out = sent(result).reshape((field_count, 2) + blocks[1:])
    keep, send = call(middle, shifted, core_pair, numbers_two, keep, swapped(send), tables)
    (result,) = call(
        end_kernel, [blocks], core_pair, numbers_two, keep, swapped(send), cells_two, tables
    )
    second_out = sent(result).reshape((field_count, 2) + blocks[1:])

    mine = jnp.where(at_first, first_out[:, 0], first_out[:, 1])
    theirs = swapped(jnp.where(at_first, first_out[:, 1], first_out[:, 0]))
    image = call_image(
        False,
        jnp.where(at_first, mine, theirs),
        jnp.where(at_first, theirs, mine),
        None,
        image_shape,
    )
    below = lax.ppermute(
        jnp.where(at_first, second_out[:, 0], second_out[:, 1]),
        "depth",
        [(d, (d + 1) % depth) for d in range(depth)],
    )
    down = lax.ppermute(
        second_out[:, 1], "depth", [(d, (d + 2) % depth) for d in range(0, depth, 2)]
    )
    left = jnp.where(at_first, down, below)
    right = jnp.where(at_first, below, second_out[:, 0])
    image = call_image(True, left, right, image, image_shape)
    inner = slice(half_lags, half_lags + rows)
    fields_out = jnp.stack(
        [
            jnp.concatenate([left[:, inner, :half], right[:, inner, :half]], axis=-1),
            jnp.concatenate([left[:, inner, half:], right[:, inner, half:]], axis=-1),
        ]
    ).reshape(fields.shape)
    return (fields_out, image[None, None])


def solution(mesh):
    in_specs = (
        P("depth", None, None, None, "lat", None),
        P(None, None, None, "lat", None),
        P("depth", None),
        P(),
        P("depth", None, None),
        P("depth", None, "lat", None),
        P("depth", None, "lat", None),
        P("depth", None, None),
    )
    out_specs = (P("depth", None, None, None, "lat", None), P("depth", None, None, "lat", None))

    def body(*args):
        fields = args[0]
        one_to_a_chip = lax.axis_size("lat") == 2 * fields.shape[2] * fields.shape[3]
        square = fields.shape[4] * lax.axis_size("lat") == fields.shape[5]
        if one_to_a_chip and square and lax.axis_size("depth") % 2 == 0:
            return chip_shards(*args)
        return shards(*args)

    return jax.shard_map(body, mesh=mesh, in_specs=in_specs, out_specs=out_specs, check_vma=False)
```

profile of v0, /device:TPU:0, one launch (start us, length us, event | category | flops | bytes accessed | tf_op | source)
XLA Modules:
  0.0 234.3 jit_solution(16840250990266225373)
XLA Ops:
  3.5 7.4 %all-to-all-start.2 = ((f32[8,64,512]{2,1,0:T(8,128)}), f32[8,64,512]{2,1,0:T(8,128)S(1)}, u32[]{:S(2)}, u32[]{:S(2)}) async-start(f32[8,64,512]{2,1,0:T(8,128)} %bitcast.32), calls=%async_computation.2 | async-start | bytes 2097152 | tf_op jit(solution)/shard_map/all_to_all | solution.py:504
  11.6 5.0 %select_bitcast_fusion.3 = f32[1,64,512]{2,1,0:T(8,128)S(1)} fusion(s32[1,1,64,512]{3,2,1,0:T(8,128)S(1)} %copy-done.2, f32[]{:T(128)} %bitcast.17, f32[]{:T(128)} %bitcast.18, f32[]{:T(128)} %bitcast.19, f32[]{:T(128)} %bitcast.20, f32[]{:T(128)} %bitcast.21, f32[]{:T(128)} %bitcast.24, f32[]{:T(128)} %bitcast.23, f32[]{:T(128)} %bitcast.22), kind=kLoop, calls=%fused_computation.35 | loop fusion | flops 524288 | bytes 262176 | tf_op jit(solution)/shard_map/jit(_where)/select_n | solution.py:520
  16.7 3.4 %collective-permute-start.9 = (f32[2,64,256]{2,1,0:T(8,128)S(1)}, f32[2,64,256]{2,1,0:T(8,128)S(1)}, u32[]{:S(2)}, u32[]{:S(2)}) collective-permute-start(f32[2,64,256]{2,1,0:T(8,128)S(1)} %get-tuple-element.21), channel_id=1, source_target_pairs={{16,0},{0,16},{17,1},{1,17},{18,2},{2,18},{19,3},{3,19},{20,4},{4,... | collective-permute-start | bytes 393224 | tf_op jit(solution)/shard_map/ppermute | solution.py:531
  24.1 12.6 %all-to-all-done.2 = f32[8,64,512]{2,1,0:T(8,128)S(1)} async-done(((f32[8,64,512]{2,1,0:T(8,128)}), f32[8,64,512]{2,1,0:T(8,128)S(1)}, u32[]{:S(2)}, u32[]{:S(2)}) %all-to-all-start.2) | async-done | bytes 1048608 | tf_op jit(solution)/shard_map/all_to_all | solution.py:504
  38.0 3.6 %all-to-all-start.1 = ((f32[8,2,64,256]{3,2,1,0:T(8,128)}), f32[8,2,64,256]{3,2,1,0:T(8,128)S(1)}, u32[]{:S(2)}, u32[]{:S(2)}) async-start(f32[8,2,64,256]{3,2,1,0:T(8,128)} %bitcast.28), calls=%async_computation.1 | async-start | bytes 2097152 | tf_op jit(solution)/shard_map/all_to_all | solution.py:504
  45.0 22.6 %all-to-all-done.1.cells_ref = f32[8,2,64,256]{3,2,1,0:T(8,128)S(1)} async-done(((f32[8,2,64,256]{3,2,1,0:T(8,128)}), f32[8,2,64,256]{3,2,1,0:T(8,128)S(1)}, u32[]{:S(2)}, u32[]{:S(2)}) %all-to-all-start.1) | async-done | bytes 1048608 | tf_op jit(solution)/shard_map/all_to_all | solution.py:504
  67.6 3.6 %all-to-all-start = ((f32[8,64,512]{2,1,0:T(8,128)}), f32[8,64,512]{2,1,0:T(8,128)S(1)}, u32[]{:S(2)}, u32[]{:S(2)}) async-start(f32[8,64,512]{2,1,0:T(8,128)} %bitcast.14), calls=%async_computation | async-start | bytes 2097152 | tf_op jit(solution)/shard_map/all_to_all | solution.py:504
  71.2 25.9 %all-to-all-done = f32[8,64,512]{2,1,0:T(8,128)S(1)} async-done(((f32[8,64,512]{2,1,0:T(8,128)}), f32[8,64,512]{2,1,0:T(8,128)S(1)}, u32[]{:S(2)}, u32[]{:S(2)}) %all-to-all-start) | async-done | bytes 1048608 | tf_op jit(solution)/shard_map/all_to_all | solution.py:504
  98.3 3.8 %all-to-all-start.3 = ((f32[8,2,64,256]{3,2,1,0:T(8,128)}), f32[8,2,64,256]{3,2,1,0:T(8,128)S(1)}, u32[]{:S(2)}, u32[]{:S(2)}) async-start(f32[8,2,64,256]{3,2,1,0:T(8,128)} %bitcast.35), calls=%async_computation.3 | async-start | bytes 2097152 | tf_op jit(solution)/shard_map/all_to_all | solution.py:504
  102.1 3.4 %collective-permute-start.1 = (f32[4]{0:T(128)S(1)}, f32[4]{0:T(128)S(1)}, u32[]{:S(2)}, u32[]{:S(2)}) collective-permute-start(f32[4]{0:T(128)S(1)} %pad_maximum_fusion.10), channel_id=1, source_target_pairs={{16,0},{0,16},{17,1},{1,17},{18,2},{2,18},{19,3},{3,19},{20,4},{4,... | collective-permute-start | bytes 56 | tf_op jit(solution)/shard_map/ppermute | solution.py:531
  107.2 3.4 %shard_map.104 = (f32[256,512]{1,0:T(8,128)S(1)}, f32[256,512]{1,0:T(8,128)S(1)}) custom-call(s32[2]{0:T(128)S(1)} %pad_add_fusion.core_ref, f32[512,512]{1,0:T(8,128)S(1)} %bitcast.94, bf16[4,512,512]{2,1,0:T(8,128)(2,1)} %constant.73.clone.tables_ref), custom_call_target="tpu_custom_call" | custom-call | tf_op jit(solution)/shard_map/pallas_call | solution.py:452
  112.6 11.4 %shard_map.105 = (f32[2,256,512]{2,1,0:T(8,128)S(1)}, f32[2,256,512]{2,1,0:T(8,128)S(1)}) custom-call(s32[2]{0:T(128)S(1)} %pad_add_fusion.core_ref, f32[4]{0:T(128)S(1)} %pad_maximum_fusion.12.numbers_ref, f32[256,512]{1,0:T(8,128)S(1)} %get-tuple-element.11.own_ref, f32[256,512]{1,0:T(8,128)S(1)} %collective-permute-done.4.other_ref, ...), custom_call_target="tpu_custom_call" | custom-call | tf_op jit(solution)/shard_map/pallas_call | solution.py:452
  124.2 2.5 %collective-permute-done.5.other_ref = f32[2,256,512]{2,1,0:T(8,128)S(1)} collective-permute-done((f32[2,256,512]{2,1,0:T(8,128)S(1)}, f32[2,256,512]{2,1,0:T(8,128)S(1)}, u32[]{:S(2)}, u32[]{:S(2)}) %collective-permute-start.5) | collective-permute-done | bytes 1048608 | tf_op jit(solution)/shard_map/ppermute | solution.py:501
  126.8 10.7 %shard_map.106 = (f32[8,80,512]{2,1,0:T(8,128)}, f32[256,512]{1,0:T(8,128)S(1)}, f32[256,512]{1,0:T(8,128)S(1)}) custom-call(s32[2]{0:T(128)S(1)} %pad_add_fusion.core_ref, f32[4]{0:T(128)S(1)} %pad_maximum_fusion.12.numbers_ref, f32[2,256,512]{2,1,0:T(8,128)S(1)} %get-tuple-element.13.own_ref, f32[2,256,512]{2,1,0:T(8,128)S(1)} %collective-permute-done.5.other_ref, ...), custom_call_target="tpu_custom_call" | custom-call | tf_op jit(solution)/shard_map/pallas_call | solution.py:452
  137.5 6.0 %all-to-all-start.5 = ((f32[8,80,512]{2,1,0:T(8,128)}), f32[8,80,512]{2,1,0:T(8,128)}, u32[]{:S(2)}, u32[]{:S(2)}) async-start(f32[8,80,512]{2,1,0:T(8,128)} %get-tuple-element.19), calls=%async_computation.5 | async-start | bytes 2621440 | tf_op jit(solution)/shard_map/all_to_all | solution.py:504
  145.4 11.5 %shard_map.107 = (f32[2,256,512]{2,1,0:T(8,128)S(1)}, f32[2,256,512]{2,1,0:T(8,128)S(1)}) custom-call(s32[2]{0:T(128)S(1)} %pad_add_fusion.core_ref, f32[4]{0:T(128)S(1)} %pad_maximum_fusion.11.numbers_ref, f32[256,512]{1,0:T(8,128)S(1)} %get-tuple-element.15.own_ref, f32[256,512]{1,0:T(8,128)S(1)} %collective-permute-done.7.other_ref, ...), custom_call_target="tpu_custom_call" | custom-call | tf_op jit(solution)/shard_map/pallas_call | solution.py:452
  157.1 2.5 %collective-permute-done.8.other_ref = f32[2,256,512]{2,1,0:T(8,128)S(1)} collective-permute-done((f32[2,256,512]{2,1,0:T(8,128)S(1)}, f32[2,256,512]{2,1,0:T(8,128)S(1)}, u32[]{:S(2)}, u32[]{:S(2)}) %collective-permute-start.8) | collective-permute-done | bytes 1048608 | tf_op jit(solution)/shard_map/ppermute | solution.py:501
  159.6 8.4 %shard_map.108 = f32[8,80,512]{2,1,0:T(8,128)} custom-call(s32[2]{0:T(128)S(1)} %pad_add_fusion.core_ref, f32[4]{0:T(128)S(1)} %pad_maximum_fusion.11.numbers_ref, f32[2,256,512]{2,1,0:T(8,128)S(1)} %get-tuple-element.17.own_ref, f32[2,256,512]{2,1,0:T(8,128)S(1)} %collective-permute-done.8.other_ref, f32[8,2,64,256]{3,2,1,0:T(8,128)S(1)} %all-to-all-done.3.cells_ref, ...), custom_call_target="tpu_custom_call" | custom-call | tf_op jit(solution)/shard_map/pallas_call | solution.py:452
  168.0 7.3 %all-to-all-done.5 = f32[8,80,512]{2,1,0:T(8,128)} async-done(((f32[8,80,512]{2,1,0:T(8,128)}), f32[8,80,512]{2,1,0:T(8,128)}, u32[]{:S(2)}, u32[]{:S(2)}) %all-to-all-start.5) | async-done | bytes 1310752 | tf_op jit(solution)/shard_map/all_to_all | solution.py:504
  175.3 3.6 %all-to-all-start.4 = ((f32[8,80,512]{2,1,0:T(8,128)}), f32[8,80,512]{2,1,0:T(8,128)S(1)}, u32[]{:S(2)}, u32[]{:S(2)}) async-start(f32[8,80,512]{2,1,0:T(8,128)} %shard_map.108), calls=%async_computation.4 | async-start | bytes 2621440 | tf_op jit(solution)/shard_map/all_to_all | solution.py:504
  180.4 30.1 %all-to-all-done.4 = f32[8,80,512]{2,1,0:T(8,128)S(1)} async-done(((f32[8,80,512]{2,1,0:T(8,128)}), f32[8,80,512]{2,1,0:T(8,128)S(1)}, u32[]{:S(2)}, u32[]{:S(2)}) %all-to-all-start.4) | async-done | bytes 1310752 | tf_op jit(solution)/shard_map/all_to_all | solution.py:504
  210.6 2.4 %collective-permute-start.11 = (f32[4,80,512]{2,1,0:T(8,128)S(1)}, f32[4,80,512]{2,1,0:T(8,128)S(1)}, u32[]{:S(2)}, u32[]{:S(2)}) collective-permute-start(f32[4,80,512]{2,1,0:T(8,128)S(1)} %slice_bitcast_fusion.3), channel_id=1, source_target_pairs={{0,16},{16,0},{1,17},{17,1},{2,18},{18,2},{3,19},{19,3},{4,20},{20... | collective-permute-start | bytes 1966088 | tf_op jit(solution)/shard_map/ppermute | solution.py:621
  215.9 14.2 %collective-permute-done.11 = f32[4,80,512]{2,1,0:T(8,128)S(1)} collective-permute-done((f32[4,80,512]{2,1,0:T(8,128)S(1)}, f32[4,80,512]{2,1,0:T(8,128)S(1)}, u32[]{:S(2)}, u32[]{:S(2)}) %collective-permute-start.11) | collective-permute-done | bytes 655392 | tf_op jit(solution)/shard_map/ppermute | solution.py:621
  230.5 2.7 %shard_map.110 = f32[16,64,512]{2,1,0:T(8,128)} custom-call(f32[4,80,512]{2,1,0:T(8,128)S(1)} %get-tuple-element.33.first_ref, f32[4,80,512]{2,1,0:T(8,128)S(1)} %get-tuple-element.34.second_ref, f32[16,64,512]{2,1,0:T(8,128)S(1)} %shard_map.109.refs_0_), custom_call_target="tpu_custom_call" | custom-call | tf_op jit(solution)/shard_map/pallas_call | solution.py:467
  (74 shorter events, 23.7 us)
Async XLA Ops:
  3.5 8.1 %copy-start.2 = (s32[1,1,64,512]{3,2,1,0:T(8,128)S(1)}, s32[1,1,64,512]{3,2,1,0:T(8,128)}, u32[]{:S(2)}) copy-start(s32[1,1,64,512]{3,2,1,0:T(8,128)} %param.15) | copy-start | bytes 393220
  3.5 13.1 %copy-start.3 = (f32[1,1,64,512]{3,2,1,0:T(8,128)S(1)}, f32[1,1,64,512]{3,2,1,0:T(8,128)}, u32[]{:S(2)}) copy-start(f32[1,1,64,512]{3,2,1,0:T(8,128)} %param.14) | copy-start | bytes 393220
  3.5 33.2 %all-to-all-start.2 = ((f32[8,64,512]{2,1,0:T(8,128)}), f32[8,64,512]{2,1,0:T(8,128)S(1)}, u32[]{:S(2)}, u32[]{:S(2)}) async-start(f32[8,64,512]{2,1,0:T(8,128)} %bitcast.32), calls=%async_computation.2 | async-start | bytes 2097152 | tf_op jit(solution)/shard_map/all_to_all | solution.py:504
  16.7 6.9 %collective-permute-start.9 = (f32[2,64,256]{2,1,0:T(8,128)S(1)}, f32[2,64,256]{2,1,0:T(8,128)S(1)}, u32[]{:S(2)}, u32[]{:S(2)}) collective-permute-start(f32[2,64,256]{2,1,0:T(8,128)S(1)} %get-tuple-element.21), channel_id=1, source_target_pairs={{16,0},{0,16},{17,1},{1,17},{18,2},{2,18},{19,3},{3,19},{20,4},{4,... | collective-permute-start | bytes 393224 | tf_op jit(solution)/shard_map/ppermute | solution.py:531
  20.1 3.9 %collective-permute-start.10 = (f32[2,64,256]{2,1,0:T(8,128)S(1)}, f32[2,64,256]{2,1,0:T(8,128)S(1)}, u32[]{:S(2)}, u32[]{:S(2)}) collective-permute-start(f32[2,64,256]{2,1,0:T(8,128)S(1)} %get-tuple-element.22), channel_id=1, source_target_pairs={{16,8},{0,24},{17,9},{1,25},{18,10},{2,26},{19,11},{3,27},{20,12},... | collective-permute-start | bytes 393224 | tf_op jit(solution)/shard_map/ppermute | solution.py:532
  21.4 2.6 %collective-permute-start.6 = (f32[2,64,256]{2,1,0:T(8,128)S(1)}, f32[2,64,256]{2,1,0:T(8,128)S(1)}, u32[]{:S(2)}, u32[]{:S(2)}) collective-permute-start(f32[2,64,256]{2,1,0:T(8,128)S(1)} %get-tuple-element.20), channel_id=1, source_target_pairs={{0,8},{8,0},{16,24},{24,16},{1,9},{9,1},{17,25},{25,17},{2,10},{10... | collective-permute-start | bytes 393224 | tf_op jit(solution)/shard_map/ppermute | solution.py:501
  38.0 29.5 %all-to-all-start.1 = ((f32[8,2,64,256]{3,2,1,0:T(8,128)}), f32[8,2,64,256]{3,2,1,0:T(8,128)S(1)}, u32[]{:S(2)}, u32[]{:S(2)}) async-start(f32[8,2,64,256]{3,2,1,0:T(8,128)} %bitcast.28), calls=%async_computation.1 | async-start | bytes 2097152 | tf_op jit(solution)/shard_map/all_to_all | solution.py:504
  41.7 2.0 collective-permute-start.3
  45.0 26.3 %copy-start.6 = (s32[1,2]{1,0:T(1,128)S(1)}, s32[1,2]{1,0:T(1,128)}, u32[]{:S(2)}) copy-start(s32[1,2]{1,0:T(1,128)} %param.11) | copy-start | bytes 28
  67.6 30.7 %copy-start.1 = (f32[8,2,64,256]{3,2,1,0:T(8,128)}, f32[8,2,64,256]{3,2,1,0:T(8,128)S(1)}, u32[]{:S(2)}) copy-start(f32[8,2,64,256]{3,2,1,0:T(8,128)S(1)} %all-to-all-done.1.cells_ref) | copy-start | bytes 3145732
  67.6 29.6 %all-to-all-start = ((f32[8,64,512]{2,1,0:T(8,128)}), f32[8,64,512]{2,1,0:T(8,128)S(1)}, u32[]{:S(2)}, u32[]{:S(2)}) async-start(f32[8,64,512]{2,1,0:T(8,128)} %bitcast.14), calls=%async_computation | async-start | bytes 2097152 | tf_op jit(solution)/shard_map/all_to_all | solution.py:504
  98.3 39.2 %all-to-all-start.3 = ((f32[8,2,64,256]{3,2,1,0:T(8,128)}), f32[8,2,64,256]{3,2,1,0:T(8,128)S(1)}, u32[]{:S(2)}, u32[]{:S(2)}) async-start(f32[8,2,64,256]{3,2,1,0:T(8,128)} %bitcast.35), calls=%async_computation.3 | async-start | bytes 2097152 | tf_op jit(solution)/shard_map/all_to_all | solution.py:504
  102.1 8.6 %collective-permute-start = (f32[4]{0:T(128)S(1)}, f32[4]{0:T(128)S(1)}, u32[]{:S(2)}, u32[]{:S(2)}) collective-permute-start(f32[4]{0:T(128)S(1)} %pad_maximum_fusion.10), channel_id=1, source_target_pairs={{0,8},{8,0},{16,24},{24,16},{1,9},{9,1},{17,25},{25,17},{2,10},{10... | collective-permute-start | bytes 56 | tf_op jit(solution)/shard_map/ppermute | solution.py:501
  102.1 8.6 %collective-permute-start.1 = (f32[4]{0:T(128)S(1)}, f32[4]{0:T(128)S(1)}, u32[]{:S(2)}, u32[]{:S(2)}) collective-permute-start(f32[4]{0:T(128)S(1)} %pad_maximum_fusion.10), channel_id=1, source_target_pairs={{16,0},{0,16},{17,1},{1,17},{18,2},{2,18},{19,3},{3,19},{20,4},{4,... | collective-permute-start | bytes 56 | tf_op jit(solution)/shard_map/ppermute | solution.py:531
  105.6 5.1 %collective-permute-start.2 = (f32[4]{0:T(128)S(1)}, f32[4]{0:T(128)S(1)}, u32[]{:S(2)}, u32[]{:S(2)}) collective-permute-start(f32[4]{0:T(128)S(1)} %pad_maximum_fusion.10), channel_id=1, source_target_pairs={{16,8},{0,24},{17,9},{1,25},{18,10},{2,26},{19,11},{3,27},{20,12},... | collective-permute-start | bytes 56 | tf_op jit(solution)/shard_map/ppermute | solution.py:532
  110.6 2.0 collective-permute-start.4
  124.0 2.7 %collective-permute-start.5 = (f32[2,256,512]{2,1,0:T(8,128)S(1)}, f32[2,256,512]{2,1,0:T(8,128)S(1)}, u32[]{:S(2)}, u32[]{:S(2)}) collective-permute-start(f32[2,256,512]{2,1,0:T(8,128)S(1)} %get-tuple-element.14), channel_id=1, source_target_pairs={{0,8},{8,0},{16,24},{24,16},{1,9},{9,1},{17,25},{25,17},{2,10},{10... | collective-permute-start | bytes 3145736 | tf_op jit(solution)/shard_map/ppermute | solution.py:501
  137.5 37.8 %all-to-all-start.5 = ((f32[8,80,512]{2,1,0:T(8,128)}), f32[8,80,512]{2,1,0:T(8,128)}, u32[]{:S(2)}, u32[]{:S(2)}) async-start(f32[8,80,512]{2,1,0:T(8,128)} %get-tuple-element.19), calls=%async_computation.5 | async-start | bytes 2621440 | tf_op jit(solution)/shard_map/all_to_all | solution.py:504
  143.5 1.9 collective-permute-start.7
  156.9 2.7 %collective-permute-start.8 = (f32[2,256,512]{2,1,0:T(8,128)S(1)}, f32[2,256,512]{2,1,0:T(8,128)S(1)}, u32[]{:S(2)}, u32[]{:S(2)}) collective-permute-start(f32[2,256,512]{2,1,0:T(8,128)S(1)} %get-tuple-element.18), channel_id=1, source_target_pairs={{0,8},{8,0},{16,24},{24,16},{1,9},{9,1},{17,25},{25,17},{2,10},{10... | collective-permute-start | bytes 3145736 | tf_op jit(solution)/shard_map/ppermute | solution.py:501
  175.3 35.2 %all-to-all-start.4 = ((f32[8,80,512]{2,1,0:T(8,128)}), f32[8,80,512]{2,1,0:T(8,128)S(1)}, u32[]{:S(2)}, u32[]{:S(2)}) async-start(f32[8,80,512]{2,1,0:T(8,128)} %shard_map.108), calls=%async_computation.4 | async-start | bytes 2621440 | tf_op jit(solution)/shard_map/all_to_all | solution.py:504
  180.3 32.8 %collective-permute-start.13 = (f32[4,80,512]{2,1,0:T(8,128)S(1)}, f32[4,80,512]{2,1,0:T(8,128)S(1)}, u32[]{:S(2)}, u32[]{:S(2)}) collective-permute-start(f32[4,80,512]{2,1,0:T(8,128)S(1)} %select_bitcast_fusion), channel_id=1, source_target_pairs={{0,8},{8,0},{16,24},{24,16},{1,9},{9,1},{17,25},{25,17},{2,10},{10... | collective-permute-start | bytes 1966088 | tf_op jit(solution)/shard_map/ppermute | solution.py:501
  210.6 19.5 %collective-permute-start.11 = (f32[4,80,512]{2,1,0:T(8,128)S(1)}, f32[4,80,512]{2,1,0:T(8,128)S(1)}, u32[]{:S(2)}, u32[]{:S(2)}) collective-permute-start(f32[4,80,512]{2,1,0:T(8,128)S(1)} %slice_bitcast_fusion.3), channel_id=1, source_target_pairs={{0,16},{16,0},{1,17},{17,1},{2,18},{18,2},{3,19},{19,3},{4,20},{20... | collective-permute-start | bytes 1966088 | tf_op jit(solution)/shard_map/ppermute | solution.py:621
  213.1 17.1 %collective-permute-start.12 = (f32[4,80,512]{2,1,0:T(8,128)S(1)}, f32[4,80,512]{2,1,0:T(8,128)S(1)}, u32[]{:S(2)}, u32[]{:S(2)}) collective-permute-start(f32[4,80,512]{2,1,0:T(8,128)S(1)} %fusion.1), channel_id=1, source_target_pairs={{0,8},{8,16},{16,24},{24,0},{1,9},{9,17},{17,25},{25,1},{2,10},{10... | collective-permute-start | bytes 1966088 | tf_op jit(solution)/shard_map/ppermute | solution.py:616
  (4 other events, 16.1 us)
where the time goes:
time: 235 us; the launch traced here: 234 us
  waiting for transfers between devices  123 us (52%)
  Pallas kernels  49.3 us (21%)
  starting transfers between devices  40.8 us (17%)
  other arithmetic  13.1 us (6%)
  local copies, waits for them, and re-layouts  5.48 us (2%)
  between operations  2.38 us (1%)
    all_to_all x6, waiting for transfers between devices, sent(): lax.all_to_all(blocks, 'lat', split_axis=0, concat_axis=0, tiled=True)  98.6 us
    pallas_call x5, Pallas kernels, call(): pl.pallas_call(kernel, out_shape=[jax.ShapeDtypeStruct(shape, jnp.float32...  45.4 us
    all_to_all x6, starting transfers between devices, sent(): lax.all_to_all(blocks, 'lat', split_axis=0, concat_axis=0, tiled=True)  28 us
    ppermute x1, waiting for transfers between devices, chip_shards(): lax.ppermute(second_out[:, 1], 'depth', [(d, (d + 2) % depth) for d in ra...  14.2 us
    ppermute x8, waiting for transfers between devices, swapped(): return lax.ppermute(value, 'depth', swap)  7.8 us
    ppermute x2, starting transfers between devices, fetched(): lax.ppermute(for_first, 'depth', after_first)  6.86 us
    select_n x1, other arithmetic, chip_shards(): jnp.where(regions[0, 0] == region, region_slowness[0, 0, region], cell)  4.96 us
  transfers between devices with their start and end apart: 20, of which 13 were waited for; matrix products, arithmetic and copies ran while one was open for 5% of the time, Pallas kernels for 20%

commit v1 on v0

--- a/solution.py
+++ b/solution.py
@@ -314,7 +314,9 @@
 
 
 def start_kernel(core_ref, blocks_ref, tables_ref, keep_ref, send_ref):
-    spread_rows(core_ref[0], tables_ref, blocks_ref[...], keep_ref, send_ref)
+    rows = 2 * keep_ref.shape[0] // blocks_ref.shape[0]
+    values = blocks_ref[:, :rows].reshape(2 * keep_ref.shape[0], blocks_ref.shape[2])
+    spread_rows(core_ref[0], tables_ref, values, keep_ref, send_ref)
 
 
 def folded(positions, length):
@@ -400,15 +402,13 @@
     own_ref,
     other_ref,
     cells_ref,
-    surface_ref,
-    tables_ref,
-    blocks_ref,
-    keep_ref,
-    send_ref,
+    *refs,
 ):
+    *piece_refs, tables_ref, blocks_ref, keep_ref, send_ref = refs
     result = continued(core_ref[0], numbers_ref, own_ref, other_ref, cells_ref, tables_ref)
     put_blocks(result, blocks_ref)
-    values = jnp.where(core_ref[1] == 1, surface_ref[...], result)
+    above = jnp.concatenate([piece_ref[...] for piece_ref in piece_refs], axis=1)
+    values = jnp.where(core_ref[1] == 1, above.reshape(result.shape), result)
     spread_rows(core_ref[0], tables_ref, values, keep_ref, send_ref)
 
 
@@ -455,6 +455,11 @@
         in_specs=specs,
         out_specs=[pl.BlockSpec(memory_space=pltpu.VMEM)] * len(outs),
         compiler_params=pltpu.CompilerParams(vmem_limit_bytes=50 << 20),
+        cost_estimate=pl.CostEstimate(
+            flops=24 * math.prod(outs[-1]) * args[-1].shape[-1],
+            bytes_accessed=4 * sum(math.prod(shape) for shape in outs),
+            transcendentals=math.prod(outs[-1]),
+        ),
     )(*args)
 
 
@@ -512,7 +517,13 @@
     both = jnp.stack(
         [jnp.where(at_first, own, other), jnp.where(at_first, other, own)], axis=1
     ).reshape(lat, rows, width)
-    held = sent(both).reshape(total_rows, width)
+    surface_half, _ = halves(surface.reshape(2, field_count, rows, width))
+    surface_half = side_by_side(surface_half)
+    part = rows // depth
+    surface_part = lax.dynamic_slice_in_dim(
+        surface_half, depth_index // 2 * (2 * part), 2 * part, axis=1
+    ).reshape(lat, part, width)
+    held = sent(jnp.concatenate([both, surface_part], axis=1))
 
     region_ids = jnp.arange(REGIONS, dtype=jnp.int32)
     cell = jnp.zeros((rows, width), jnp.float32)
@@ -522,24 +533,17 @@
         [ref_slowness[0, 0], held_freqs[0].astype(jnp.float32) * omega_step]
     )
     other_numbers = swapped(numbers)
-    after_first = [((d + 2) % depth, d) for d in range(0, depth, 2)]
-    after_second = [((d + 2) % depth, d + 1) for d in range(0, depth, 2)]
-
-    def fetched(for_first, for_second):
-        return jnp.where(
-            at_first,
-            lax.ppermute(for_first, "depth", after_first),
-            lax.ppermute(for_second, "depth", after_second),
-        )
-
-    next_numbers = fetched(numbers, numbers)
     section_numbers = (
         jnp.where(at_first, numbers, other_numbers),
         jnp.where(at_first, other_numbers, numbers),
-        next_numbers,
     )
     first_numbers = jnp.where(place == 0, section_numbers[0], section_numbers[1])
-    second_numbers = jnp.where(place == 0, section_numbers[1], section_numbers[2])
+    below_chip = [
+        (d * lat + j, (d * lat + j - 1) if j % 2 else ((d - 2) % depth * lat + j + 1))
+        for d in range(depth)
+        for j in range(lat)
+    ]
+    second_numbers = lax.ppermute(first_numbers, ("depth", "lat"), below_chip)
     takes_surface = (depth_index // 2 == depth // 2 - 1) & (place == 1)
     freq = field % freq_count
     freq_ids = jnp.arange(freq_count, dtype=jnp.int32)
@@ -559,7 +563,6 @@
     cells = jnp.stack([weights[0, 0], cell])
     own_cells, other_cells = halves(cells)
     other_cells = swapped(other_cells)
-    third = fetched(cells[..., :half], cells[..., half:])
     zero = jnp.where(at_first, own_cells, other_cells)
     one = jnp.where(at_first, other_cells, own_cells)
 
@@ -569,14 +572,24 @@
             (lat,) + even.shape
         )
 
-    cells_one = sent(cell_blocks(zero, one))
-    cells_two = sent(cell_blocks(one, third))
-    surface_half, _ = halves(surface.reshape(2, field_count, rows, width))
-    surface_half = side_by_side(surface_half)
-    surface_blocks = jnp.broadcast_to(
-        surface_half[:, None], (field_count, 2, rows, width)
-    ).reshape(lat, rows, width)
-    above = sent(surface_blocks).reshape(total_rows, width)
+    blocks_one, held = lax.optimization_barrier((cell_blocks(zero, one), held))
+    cells_one = sent(blocks_one)
+    cells_two = lax.ppermute(cells_one, ("depth", "lat"), below_chip)
+
+    last = depth // 2 - 1
+    surface_part = held[:, rows:]
+    pieces = []
+    for piece in range(depth):
+        plane, side = (piece // 2, piece % 2)
+        if (plane, side) == (last, 1):
+            pieces.append(surface_part)
+            continue
+        route = [
+            ((2 * plane + c) * lat + 2 * f + side, (2 * last + c) * lat + 2 * f + 1)
+            for c in range(2)
+            for f in range(field_count)
+        ]
+        pieces.append(lax.ppermute(surface_part, ("depth", "lat"), route))
 
     spread = [(total_rows // 2, width)] * 2
     shifted = [(2, total_rows // 2, width)] * 2
@@ -594,7 +607,7 @@
         keep,
         swapped(send),
         cells_one,
-        above,
+        *pieces,
         tables,
     )
     first_out = sent(result).reshape((field_count, 2) + blocks[1:])
@@ -651,7 +664,8 @@
         fields = args[0]
         one_to_a_chip = lax.axis_size("lat") == 2 * fields.shape[2] * fields.shape[3]
         square = fields.shape[4] * lax.axis_size("lat") == fields.shape[5]
-        if one_to_a_chip and square and lax.axis_size("depth") % 2 == 0:
+        depth = lax.axis_size("depth")
+        if one_to_a_chip and square and depth % 2 == 0 and fields.shape[4] % (8 * depth) == 0:
             return chip_shards(*args)
         return shards(*args)
 

time: 235 us -> 210 us (0.89)
  waiting for transfers between devices: 123 us -> 92.4 us
  starting transfers between devices: 40.8 us -> 48.3 us
  local copies, waits for them, and re-layouts: 5.48 us -> 2.11 us
    all_to_all x6 -> x4, waiting for transfers between devices: 98.6 us -> 53.7 us  [sent(): lax.all_to_all(blocks, 'lat', split_axis=0, concat_axis=0, tiled=True)]
    ppermute x4 -> x5, waiting for transfers between devices: 2.49 us -> 24.9 us  [the longest x1 15.6 us: chip_shards(): cells_two = lax.ppermute(cells_one, ('depth', 'lat'), below_chip)]
    ppermute x1, waiting for transfers between devices: 14.2 us -> 2.48 us  [chip_shards(): lax.ppermute(second_out[:, 1], 'depth', [(d, (d + 2) % depth) for d in ra...]
    ppermute x1, waiting for transfers between devices: 0.01 us -> 8.85 us  [chip_shards(): lax.ppermute(jnp.where(at_first, second_out[:, 0], second_out[:, 1]), 'de...]
    ppermute x8, waiting for transfers between devices: 7.8 us -> 2.52 us  [swapped(): return lax.ppermute(value, 'depth', swap)]
    ppermute x4 -> x5, starting transfers between devices: 9.62 us -> 14.9 us  [the longest x3 7.53 us: chip_shards(): pieces.append(lax.ppermute(surface_part, ('depth', 'lat'), route))]
    all_to_all x6 -> x4, starting transfers between devices: 28 us -> 28.9 us  [sent(): lax.all_to_all(blocks, 'lat', split_axis=0, concat_axis=0, tiled=True)]
  transfers between devices with their start and end apart: 20 -> 19, of which waited for: 13 -> 10; matrix products, arithmetic and copies ran while one was open for 5% -> 6% of each run, Pallas kernels for 20% -> 17%
where the time goes in v1:
time: 210 us; the launch traced here: 209 us
  waiting for transfers between devices  92.4 us (44%)
  Pallas kernels  49.1 us (23%)
  starting transfers between devices  48.3 us (23%)
  other arithmetic  14.8 us (7%)
  between operations  2.3 us (1%)
  local copies, waits for them, and re-layouts  2.11 us (1%)
    all_to_all x4, waiting for transfers between devices, sent(): lax.all_to_all(blocks, 'lat', split_axis=0, concat_axis=0, tiled=True)  53.7 us
    pallas_call x5, Pallas kernels, call(): pl.pallas_call(kernel, out_shape=[jax.ShapeDtypeStruct(shape, jnp.float32...  45.1 us
    all_to_all x4, starting transfers between devices, sent(): lax.all_to_all(blocks, 'lat', split_axis=0, concat_axis=0, tiled=True)  28.9 us
    ppermute x1, waiting for transfers between devices, chip_shards(): cells_two = lax.ppermute(cells_one, ('depth', 'lat'), below_chip)  15.6 us
    ppermute x1, waiting for transfers between devices, chip_shards(): lax.ppermute(jnp.where(at_first, second_out[:, 0], second_out[:, 1]), 'de...  8.85 us
    ppermute x3, starting transfers between devices, chip_shards(): pieces.append(lax.ppermute(surface_part, ('depth', 'lat'), route))  7.53 us
    ppermute x3, waiting for transfers between devices, chip_shards(): pieces.append(lax.ppermute(surface_part, ('depth', 'lat'), route))  5.91 us
    select_n x1, other arithmetic, chip_shards(): jnp.where(regions[0, 0] == region, region_slowness[0, 0, region], cell)  5.01 us
  transfers between devices with their start and end apart: 19, of which 10 were waited for; matrix products, arithmetic and copies ran while one was open for 6% of the time, Pallas kernels for 17%

profile of v1, /device:TPU:0, one launch (start us, length us, event | category | flops | bytes accessed | tf_op | source)
XLA Modules:
  0.0 209.0 jit_solution(298068763075871694)
XLA Ops:
  0.6 1.7 slice_select_fusion.2
  6.0 7.3 %all-to-all-start = ((f32[8,80,512]{2,1,0:T(8,128)}), f32[8,80,512]{2,1,0:T(8,128)S(1)}, u32[]{:S(2)}, u32[]{:S(2)}) async-start(f32[8,80,512]{2,1,0:T(8,128)} %pad_maximum_fusion), calls=%async_computation | async-start | bytes 2621440 | tf_op jit(solution)/shard_map/all_to_all | solution.py:509
  14.0 5.0 %select_bitcast_fusion.3 = f32[1,64,512]{2,1,0:T(8,128)S(1)} fusion(s32[1,1,64,512]{3,2,1,0:T(8,128)S(1)} %copy-done.1, f32[]{:T(128)} %bitcast.8, f32[]{:T(128)} %bitcast.9, f32[]{:T(128)} %bitcast.10, f32[]{:T(128)} %bitcast.11, f32[]{:T(128)} %bitcast.12, f32[]{:T(128)} %bitcast.15, f32[]{:T(128)} %bitcast.14, f32[]{:T(128)} %bitcast.13), kind=kLoop, calls=%fused_computation.37 | loop fusion | flops 524288 | bytes 262176 | tf_op jit(solution)/shard_map/jit(_where)/select_n | solution.py:531
  20.5 24.5 %all-to-all-done.blocks_ref = f32[8,80,512]{2,1,0:T(8,128)S(1)} async-done(((f32[8,80,512]{2,1,0:T(8,128)}), f32[8,80,512]{2,1,0:T(8,128)S(1)}, u32[]{:S(2)}, u32[]{:S(2)}) %all-to-all-start) | async-done | bytes 1310752 | tf_op jit(solution)/shard_map/all_to_all | solution.py:509
  46.1 4.3 %all-to-all-start.1 = ((f32[8,2,64,256]{3,2,1,0:T(8,128)}), f32[8,2,64,256]{3,2,1,0:T(8,128)}, u32[]{:S(2)}, u32[]{:S(2)}) async-start(f32[8,2,64,256]{3,2,1,0:T(8,128)} %bitcast.19), calls=%async_computation.1 | async-start | bytes 2097152 | tf_op jit(solution)/shard_map/all_to_all | solution.py:509
  50.3 3.4 %shard_map.104 = (f32[256,512]{1,0:T(8,128)S(1)}, f32[256,512]{1,0:T(8,128)S(1)}) custom-call(s32[2]{0:T(128)S(1)} %pad_add_fusion.core_ref, f32[8,80,512]{2,1,0:T(8,128)S(1)} %all-to-all-done.blocks_ref, bf16[4,512,512]{2,1,0:T(8,128)(2,1)} %constant.79.clone.tables_ref.refs_4_), custom_call_target="tpu_custom_call" | custom-call | flops 1610612736 | bytes 1048576 | tf_op jit(solution)/shard_map/pallas_call | solution.py:452
  55.7 11.5 %shard_map.105 = (f32[2,256,512]{2,1,0:T(8,128)S(1)}, f32[2,256,512]{2,1,0:T(8,128)S(1)}) custom-call(s32[2]{0:T(128)S(1)} %pad_add_fusion.core_ref, f32[4]{0:T(128)S(1)} %pad_maximum_fusion.11.numbers_ref, f32[256,512]{1,0:T(8,128)S(1)} %get-tuple-element.14.own_ref, f32[256,512]{1,0:T(8,128)S(1)} %collective-permute-done.4.other_ref, ...), custom_call_target="tpu_custom_call" | custom-call | flops 3221225472 | bytes 2097152 | tf_op jit(solution)/shard_map/pallas_call | solution.py:452
  68.8 6.2 %collective-permute-start.6 = (f32[8,16,512]{2,1,0:T(8,128)S(1)}, f32[8,16,512]{2,1,0:T(8,128)S(1)}, u32[]{:S(2)}, u32[]{:S(2)}) collective-permute-start(f32[8,16,512]{2,1,0:T(8,128)S(1)} %slice.127.refs_3_), channel_id=1, source_target_pairs={{0,17},{2,19},{4,21},{6,23},{8,25},{10,27},{12,29},{14,31}} | collective-permute-start | bytes 786440 | tf_op jit(solution)/shard_map/ppermute | solution.py:592
  75.0 5.9 %collective-permute-done.6.refs_0_ = f32[8,16,512]{2,1,0:T(8,128)S(1)} collective-permute-done((f32[8,16,512]{2,1,0:T(8,128)S(1)}, f32[8,16,512]{2,1,0:T(8,128)S(1)}, u32[]{:S(2)}, u32[]{:S(2)}) %collective-permute-start.6) | collective-permute-done | bytes 262176 | tf_op jit(solution)/shard_map/ppermute | solution.py:592
  80.9 10.5 %shard_map.106 = (f32[8,80,512]{2,1,0:T(8,128)}, f32[256,512]{1,0:T(8,128)S(1)}, f32[256,512]{1,0:T(8,128)S(1)}) custom-call(s32[2]{0:T(128)S(1)} %pad_add_fusion.core_ref, f32[4]{0:T(128)S(1)} %pad_maximum_fusion.11.numbers_ref, f32[2,256,512]{2,1,0:T(8,128)S(1)} %get-tuple-element.16.own_ref, f32[2,256,512]{2,1,0:T(8,128)} %collective-permute-done.5.other_ref, ...), custom_call_target="tpu_custom_call" | custom-call | flops 1610612736 | bytes 2359296 | tf_op jit(solution)/shard_map/pallas_call | solution.py:452
  91.4 9.0 %all-to-all-start.3 = ((f32[8,80,512]{2,1,0:T(8,128)}), f32[8,80,512]{2,1,0:T(8,128)}, u32[]{:S(2)}, u32[]{:S(2)}) async-start(f32[8,80,512]{2,1,0:T(8,128)} %get-tuple-element.23), calls=%async_computation.3 | async-start | bytes 2621440 | tf_op jit(solution)/shard_map/all_to_all | solution.py:509
  101.0 3.9 %collective-permute-start.1 = (f32[4]{0:T(128)S(1)}, f32[4]{0:T(128)S(1)}, u32[]{:S(2)}, u32[]{:S(2)}) collective-permute-start(f32[4]{0:T(128)S(1)} %broadcast_select_fusion.5), channel_id=1, source_target_pairs={{0,17},{1,0},{2,19},{3,2},{4,21},{5,4},{6,23},{7,6},{8,25},{9,8},{... | collective-permute-start | bytes 56 | tf_op jit(solution)/shard_map/ppermute | solution.py:546
  106.2 3.3 %collective-permute-done.1 = f32[4]{0:T(128)S(1)} collective-permute-done((f32[4]{0:T(128)S(1)}, f32[4]{0:T(128)S(1)}, u32[]{:S(2)}, u32[]{:S(2)}) %collective-permute-start.1) | collective-permute-done | bytes 48 | tf_op jit(solution)/shard_map/ppermute | solution.py:546
  109.6 3.4 %collective-permute-start.11 = (f32[8,2,64,256]{3,2,1,0:T(8,128)}, f32[8,2,64,256]{3,2,1,0:T(8,128)S(1)}, u32[]{:S(2)}, u32[]{:S(2)}) collective-permute-start(f32[8,2,64,256]{3,2,1,0:T(8,128)} %all-to-all-done.1.cells_ref), channel_id=1, source_target_pairs={{0,17},{1,0},{2,19},{3,2},{4,21},{5,4},{6,23},{7,6},{8,25},{9,8},{... | collective-permute-start | bytes 3145736 | tf_op jit(solution)/shard_map/ppermute | solution.py:577
  113.0 11.5 %shard_map.107 = (f32[2,256,512]{2,1,0:T(8,128)S(1)}, f32[2,256,512]{2,1,0:T(8,128)S(1)}) custom-call(s32[2]{0:T(128)S(1)} %pad_add_fusion.core_ref, f32[4]{0:T(128)S(1)} %pad_maximum_fusion.10.numbers_ref, f32[256,512]{1,0:T(8,128)S(1)} %get-tuple-element.19.own_ref, f32[256,512]{1,0:T(8,128)S(1)} %collective-permute-done.9.other_ref, ...), custom_call_target="tpu_custom_call" | custom-call | flops 3221225472 | bytes 2097152 | tf_op jit(solution)/shard_map/pallas_call | solution.py:452
  124.6 15.6 %collective-permute-done.11.cells_ref = f32[8,2,64,256]{3,2,1,0:T(8,128)S(1)} collective-permute-done((f32[8,2,64,256]{3,2,1,0:T(8,128)}, f32[8,2,64,256]{3,2,1,0:T(8,128)S(1)}, u32[]{:S(2)}, u32[]{:S(2)}) %collective-permute-start.11) | collective-permute-done | bytes 1048608 | tf_op jit(solution)/shard_map/ppermute | solution.py:577
  140.2 8.3 %shard_map.108 = f32[8,80,512]{2,1,0:T(8,128)} custom-call(s32[2]{0:T(128)S(1)} %pad_add_fusion.core_ref, f32[4]{0:T(128)S(1)} %pad_maximum_fusion.10.numbers_ref, f32[2,256,512]{2,1,0:T(8,128)S(1)} %get-tuple-element.21.own_ref, f32[2,256,512]{2,1,0:T(8,128)S(1)} %collective-permute-done.10.other_ref, ...), custom_call_target="tpu_custom_call" | custom-call | flops 4026531840 | bytes 1310720 | tf_op jit(solution)/shard_map/pallas_call | solution.py:452
  148.6 8.4 %all-to-all-start.2 = ((f32[8,80,512]{2,1,0:T(8,128)}), f32[8,80,512]{2,1,0:T(8,128)S(1)}, u32[]{:S(2)}, u32[]{:S(2)}) async-start(f32[8,80,512]{2,1,0:T(8,128)} %shard_map.108), calls=%async_computation.2 | async-start | bytes 2621440 | tf_op jit(solution)/shard_map/all_to_all | solution.py:509
  158.4 29.2 %all-to-all-done.2 = f32[8,80,512]{2,1,0:T(8,128)S(1)} async-done(((f32[8,80,512]{2,1,0:T(8,128)}), f32[8,80,512]{2,1,0:T(8,128)S(1)}, u32[]{:S(2)}, u32[]{:S(2)}) %all-to-all-start.2) | async-done | bytes 1310752 | tf_op jit(solution)/shard_map/all_to_all | solution.py:509
  187.8 2.9 %collective-permute-start.12 = (f32[4,80,512]{2,1,0:T(8,128)S(1)}, f32[4,80,512]{2,1,0:T(8,128)S(1)}, u32[]{:S(2)}, u32[]{:S(2)}) collective-permute-start(f32[4,80,512]{2,1,0:T(8,128)S(1)} %slice_bitcast_fusion.3), channel_id=1, source_target_pairs={{0,16},{16,0},{1,17},{17,1},{2,18},{18,2},{3,19},{19,3},{4,20},{20... | collective-permute-start | bytes 1966088 | tf_op jit(solution)/shard_map/ppermute | solution.py:634
  190.8 1.5 bitcast_select_fusion
  193.5 8.8 %collective-permute-done.13 = f32[4,80,512]{2,1,0:T(8,128)S(1)} collective-permute-done((f32[4,80,512]{2,1,0:T(8,128)S(1)}, f32[4,80,512]{2,1,0:T(8,128)S(1)}, u32[]{:S(2)}, u32[]{:S(2)}) %collective-permute-start.13) | collective-permute-done | bytes 655392 | tf_op jit(solution)/shard_map/ppermute | solution.py:629
  202.4 2.5 %collective-permute-done.12 = f32[4,80,512]{2,1,0:T(8,128)S(1)} collective-permute-done((f32[4,80,512]{2,1,0:T(8,128)S(1)}, f32[4,80,512]{2,1,0:T(8,128)S(1)}, u32[]{:S(2)}, u32[]{:S(2)}) %collective-permute-start.12) | collective-permute-done | bytes 655392 | tf_op jit(solution)/shard_map/ppermute | solution.py:634
  205.1 2.7 %shard_map.110 = f32[16,64,512]{2,1,0:T(8,128)} custom-call(f32[4,80,512]{2,1,0:T(8,128)S(1)} %get-tuple-element.34.first_ref, f32[4,80,512]{2,1,0:T(8,128)S(1)} %get-tuple-element.35.second_ref, f32[16,64,512]{2,1,0:T(8,128)S(1)} %shard_map.109.refs_0_), custom_call_target="tpu_custom_call" | custom-call | tf_op jit(solution)/shard_map/pallas_call | solution.py:472
  (68 shorter events, 15.4 us)
Async XLA Ops:
  2.4 2.1 %collective-permute-start.3 = (f32[4,64,512]{2,1,0:T(8,128)S(1)}, f32[4,64,512]{2,1,0:T(8,128)S(1)}, u32[]{:S(2)}, u32[]{:S(2)}) collective-permute-start(f32[4,64,512]{2,1,0:T(8,128)S(1)} %pad_maximum_fusion.4), channel_id=1, source_target_pairs={{0,8},{8,0},{16,24},{24,16},{1,9},{9,1},{17,25},{25,17},{2,10},{10... | collective-permute-start | bytes 1572872 | tf_op jit(solution)/shard_map/ppermute | solution.py:506
  6.0 8.0 %copy-start.1 = (s32[1,1,64,512]{3,2,1,0:T(8,128)S(1)}, s32[1,1,64,512]{3,2,1,0:T(8,128)}, u32[]{:S(2)}) copy-start(s32[1,1,64,512]{3,2,1,0:T(8,128)} %param.15) | copy-start | bytes 393220
  6.0 13.0 %copy-start = (f32[1,1,64,512]{3,2,1,0:T(8,128)S(1)}, f32[1,1,64,512]{3,2,1,0:T(8,128)}, u32[]{:S(2)}) copy-start(f32[1,1,64,512]{3,2,1,0:T(8,128)} %param.14) | copy-start | bytes 393220
  6.0 13.1 %copy-start.4 = (s32[1,2]{1,0:T(1,128)S(1)}, s32[1,2]{1,0:T(1,128)}, u32[]{:S(2)}) copy-start(s32[1,2]{1,0:T(1,128)} %param.11) | copy-start | bytes 28
  6.0 13.1 %copy-start.3 = (f32[1,1,2]{2,1,0:T(1,128)S(1)}, f32[1,1,2]{2,1,0:T(1,128)}, u32[]{:S(2)}) copy-start(f32[1,1,2]{2,1,0:T(1,128)} %param.13) | copy-start | bytes 28
  6.0 39.0 %all-to-all-start = ((f32[8,80,512]{2,1,0:T(8,128)}), f32[8,80,512]{2,1,0:T(8,128)S(1)}, u32[]{:S(2)}, u32[]{:S(2)}) async-start(f32[8,80,512]{2,1,0:T(8,128)} %pad_maximum_fusion), calls=%async_computation | async-start | bytes 2621440 | tf_op jit(solution)/shard_map/all_to_all | solution.py:509
  19.0 1.4 collective-permute-start.2
  19.2 34.6 %collective-permute-start = (f32[4]{0:T(128)S(1)}, f32[4]{0:T(128)S(1)}, u32[]{:S(2)}, u32[]{:S(2)}) collective-permute-start(f32[4]{0:T(128)S(1)} %pad_maximum_fusion.9), channel_id=1, source_target_pairs={{0,8},{8,0},{16,24},{24,16},{1,9},{9,1},{17,25},{25,17},{2,10},{10... | collective-permute-start | bytes 56 | tf_op jit(solution)/shard_map/ppermute | solution.py:506
  46.1 34.8 %all-to-all-start.1 = ((f32[8,2,64,256]{3,2,1,0:T(8,128)}), f32[8,2,64,256]{3,2,1,0:T(8,128)}, u32[]{:S(2)}, u32[]{:S(2)}) async-start(f32[8,2,64,256]{3,2,1,0:T(8,128)} %bitcast.19), calls=%async_computation.1 | async-start | bytes 2097152 | tf_op jit(solution)/shard_map/all_to_all | solution.py:509
  53.7 2.0 collective-permute-start.4
  67.2 13.7 %collective-permute-start.5 = (f32[2,256,512]{2,1,0:T(8,128)S(1)}, f32[2,256,512]{2,1,0:T(8,128)}, u32[]{:S(2)}, u32[]{:S(2)}) collective-permute-start(f32[2,256,512]{2,1,0:T(8,128)S(1)} %get-tuple-element.17), channel_id=1, source_target_pairs={{0,8},{8,0},{16,24},{24,16},{1,9},{9,1},{17,25},{25,17},{2,10},{10... | collective-permute-start | bytes 3145736 | tf_op jit(solution)/shard_map/ppermute | solution.py:506
  67.4 7.6 %collective-permute-start.8 = (f32[8,16,512]{2,1,0:T(8,128)S(1)}, f32[8,16,512]{2,1,0:T(8,128)S(1)}, u32[]{:S(2)}, u32[]{:S(2)}) collective-permute-start(f32[8,16,512]{2,1,0:T(8,128)S(1)} %slice.127.refs_3_), channel_id=1, source_target_pairs={{16,17},{18,19},{20,21},{22,23},{24,25},{26,27},{28,29},{30,31}} | collective-permute-start | bytes 786440 | tf_op jit(solution)/shard_map/ppermute | solution.py:592
  68.1 6.9 %collective-permute-start.7 = (f32[8,16,512]{2,1,0:T(8,128)S(1)}, f32[8,16,512]{2,1,0:T(8,128)S(1)}, u32[]{:S(2)}, u32[]{:S(2)}) collective-permute-start(f32[8,16,512]{2,1,0:T(8,128)S(1)} %slice.127.refs_3_), channel_id=1, source_target_pairs={{1,17},{3,19},{5,21},{7,23},{9,25},{11,27},{13,29},{15,31}} | collective-permute-start | bytes 786440 | tf_op jit(solution)/shard_map/ppermute | solution.py:592
  68.8 12.1 %collective-permute-start.6 = (f32[8,16,512]{2,1,0:T(8,128)S(1)}, f32[8,16,512]{2,1,0:T(8,128)S(1)}, u32[]{:S(2)}, u32[]{:S(2)}) collective-permute-start(f32[8,16,512]{2,1,0:T(8,128)S(1)} %slice.127.refs_3_), channel_id=1, source_target_pairs={{0,17},{2,19},{4,21},{6,23},{8,25},{10,27},{12,29},{14,31}} | collective-permute-start | bytes 786440 | tf_op jit(solution)/shard_map/ppermute | solution.py:592
  91.4 9.0 %copy-start.5 = (s32[2]{0:T(128)S(1)}, s32[2]{0:T(128)}, u32[]{:S(2)}) copy-start(s32[2]{0:T(128)} %param.12) | copy-start | bytes 28
  91.4 57.1 %all-to-all-start.3 = ((f32[8,80,512]{2,1,0:T(8,128)}), f32[8,80,512]{2,1,0:T(8,128)}, u32[]{:S(2)}, u32[]{:S(2)}) async-start(f32[8,80,512]{2,1,0:T(8,128)} %get-tuple-element.23), calls=%async_computation.3 | async-start | bytes 2621440 | tf_op jit(solution)/shard_map/all_to_all | solution.py:509
  100.4 12.6 %collective-permute-start.9 = (f32[256,512]{1,0:T(8,128)S(1)}, f32[256,512]{1,0:T(8,128)S(1)}, u32[]{:S(2)}, u32[]{:S(2)}) collective-permute-start(f32[256,512]{1,0:T(8,128)S(1)} %get-tuple-element.20), channel_id=1, source_target_pairs={{0,8},{8,0},{16,24},{24,16},{1,9},{9,1},{17,25},{25,17},{2,10},{10... | collective-permute-start | bytes 1572872 | tf_op jit(solution)/shard_map/ppermute | solution.py:506
  101.0 8.5 %collective-permute-start.1 = (f32[4]{0:T(128)S(1)}, f32[4]{0:T(128)S(1)}, u32[]{:S(2)}, u32[]{:S(2)}) collective-permute-start(f32[4]{0:T(128)S(1)} %broadcast_select_fusion.5), channel_id=1, source_target_pairs={{0,17},{1,0},{2,19},{3,2},{4,21},{5,4},{6,23},{7,6},{8,25},{9,8},{... | collective-permute-start | bytes 56 | tf_op jit(solution)/shard_map/ppermute | solution.py:546
  109.6 30.6 %collective-permute-start.11 = (f32[8,2,64,256]{3,2,1,0:T(8,128)}, f32[8,2,64,256]{3,2,1,0:T(8,128)S(1)}, u32[]{:S(2)}, u32[]{:S(2)}) collective-permute-start(f32[8,2,64,256]{3,2,1,0:T(8,128)} %all-to-all-done.1.cells_ref), channel_id=1, source_target_pairs={{0,17},{1,0},{2,19},{3,2},{4,21},{5,4},{6,23},{7,6},{8,25},{9,8},{... | collective-permute-start | bytes 3145736 | tf_op jit(solution)/shard_map/ppermute | solution.py:577
  124.5 15.7 %collective-permute-start.10 = (f32[2,256,512]{2,1,0:T(8,128)S(1)}, f32[2,256,512]{2,1,0:T(8,128)S(1)}, u32[]{:S(2)}, u32[]{:S(2)}) collective-permute-start(f32[2,256,512]{2,1,0:T(8,128)S(1)} %get-tuple-element.22), channel_id=1, source_target_pairs={{0,8},{8,0},{16,24},{24,16},{1,9},{9,1},{17,25},{25,17},{2,10},{10... | collective-permute-start | bytes 3145736 | tf_op jit(solution)/shard_map/ppermute | solution.py:506
  148.6 39.0 %all-to-all-start.2 = ((f32[8,80,512]{2,1,0:T(8,128)}), f32[8,80,512]{2,1,0:T(8,128)S(1)}, u32[]{:S(2)}, u32[]{:S(2)}) async-start(f32[8,80,512]{2,1,0:T(8,128)} %shard_map.108), calls=%async_computation.2 | async-start | bytes 2621440 | tf_op jit(solution)/shard_map/all_to_all | solution.py:509
  158.4 32.4 %collective-permute-start.14 = (f32[4,80,512]{2,1,0:T(8,128)S(1)}, f32[4,80,512]{2,1,0:T(8,128)S(1)}, u32[]{:S(2)}, u32[]{:S(2)}) collective-permute-start(f32[4,80,512]{2,1,0:T(8,128)S(1)} %select_bitcast_fusion), channel_id=1, source_target_pairs={{0,8},{8,0},{16,24},{24,16},{1,9},{9,1},{17,25},{25,17},{2,10},{10... | collective-permute-start | bytes 1966088 | tf_op jit(solution)/shard_map/ppermute | solution.py:506
  187.8 14.6 %collective-permute-start.13 = (f32[4,80,512]{2,1,0:T(8,128)S(1)}, f32[4,80,512]{2,1,0:T(8,128)S(1)}, u32[]{:S(2)}, u32[]{:S(2)}) collective-permute-start(f32[4,80,512]{2,1,0:T(8,128)S(1)} %fusion.1), channel_id=1, source_target_pairs={{0,8},{8,16},{16,24},{24,0},{1,9},{9,17},{17,25},{25,1},{2,10},{10... | collective-permute-start | bytes 1966088 | tf_op jit(solution)/shard_map/ppermute | solution.py:629
  187.8 17.0 %collective-permute-start.12 = (f32[4,80,512]{2,1,0:T(8,128)S(1)}, f32[4,80,512]{2,1,0:T(8,128)S(1)}, u32[]{:S(2)}, u32[]{:S(2)}) collective-permute-start(f32[4,80,512]{2,1,0:T(8,128)S(1)} %slice_bitcast_fusion.3), channel_id=1, source_target_pairs={{0,16},{16,0},{1,17},{17,1},{2,18},{18,2},{3,19},{19,3},{4,20},{20... | collective-permute-start | bytes 1966088 | tf_op jit(solution)/shard_map/ppermute | solution.py:634
  (1 other events, 7.3 us)

commit v2 on v1

--- a/solution.py
+++ b/solution.py
@@ -250,6 +250,7 @@
             )
     return (wave_state[None], jnp.stack(images)[None])
 
+
 def split_halves(value):
     high = value.astype(jnp.bfloat16)
     low = (value - high.astype(jnp.float32)).astype(jnp.bfloat16)
@@ -258,13 +259,23 @@
 
 def dft_tables(length):
     index = np.arange(length)
-    turning = 2.0 * np.pi / length * (index[:, None] * index[None, :] % length)
+    turning = 2.0 * np.pi / length * (index[: length // 4, None] * index[None, :] % length)
     tables = []
     for exact in (np.cos(turning), np.sin(turning)):
         high = exact.astype(ml_dtypes.bfloat16)
         low = (exact - high.astype(np.float64)).astype(ml_dtypes.bfloat16)
         tables += [high, low]
-    return np.stack(tables)
+    cosine, sine = (jnp.asarray(np.stack(tables[:2])), jnp.asarray(np.stack(tables[2:])))
+    turns = jnp.arange(length, dtype=jnp.int32) % 4
+    quarters = []
+    for _ in range(4):
+        quarters.append(jnp.stack([cosine, sine]))
+        swap_them = turns % 2 == 1
+        first = jnp.where(swap_them, sine, cosine)
+        second = jnp.where(swap_them, cosine, sine)
+        cosine = jnp.where((turns == 1) | (turns == 2), -first, first)
+        sine = jnp.where(turns >= 2, -second, second)
+    return jnp.concatenate(quarters, axis=2).reshape(4, length, length)
 
 
 def dot(left, right):
@@ -324,7 +335,18 @@
     return moved.astype(jnp.float32) * (2.0 * math.pi / length)
 
 
-def middle_kernel(scale, core_ref, numbers_ref, own_ref, other_ref, tables_ref, keep_ref, send_ref):
+def middle_kernel(
+    scale,
+    core_ref,
+    numbers_ref,
+    own_ref,
+    other_ref,
+    tables_ref,
+    keep_ref,
+    send_ref,
+    real_ref,
+    imag_ref,
+):
     core = core_ref[0]
     at_first = core == 0
     rows, width = own_ref.shape
@@ -339,12 +361,15 @@
         ],
         axis=0,
     )
-    real, imag = dft_right(tables_ref, values, -1.0)
+    real_ref[...], imag_ref[...] = dft_right(tables_ref, values, -1.0)
     kx = folded(lax.broadcasted_iota(jnp.int32, (rows, 1), 0) + core * rows, 2 * rows)
     ky = folded(lax.broadcasted_iota(jnp.int32, (1, width), 1), width)
     squared = kx * kx + ky * ky
     omega, sign = (numbers_ref[0], numbers_ref[1])
-    for ref_index in range(2):
+
+    @pl.loop(0, 2)
+    def _(ref_index):
+        real, imag = (real_ref[...], imag_ref[...])
         base = omega * numbers_ref[2 + ref_index]
         gap = base * base - squared
         amplitude = jnp.exp(-jnp.sqrt(jnp.maximum(-gap, 0.0))) * scale
@@ -359,22 +384,24 @@
         send_ref[ref_index] = jnp.where(at_first, second, first)
 
 
-def continued(core, numbers_ref, own_ref, other_ref, cells_ref, tables_ref):
+def continued(core, numbers_ref, own_ref, other_ref, cells_ref, tables_ref, real_ref, imag_ref):
     at_first = core == 0
     rows, width = own_ref.shape[1:]
     half = width // 2
-    fields = []
-    for ref_index in range(2):
+
+    @pl.loop(0, 2)
+    def _(ref_index):
         own, other = (own_ref[ref_index], other_ref[ref_index])
         values = jnp.concatenate(
             [jnp.where(at_first, own, other), jnp.where(at_first, other, own)], axis=0
         )
-        fields.append(dft_left(tables_ref, values, 1.0))
+        real_ref[ref_index], imag_ref[ref_index] = dft_left(tables_ref, values, 1.0)
+
     weight = cells_ref[:, 0].reshape(2 * rows, half)
     cell = cells_ref[:, 1].reshape(2 * rows, half)
     rest = 1.0 - weight
-    real = weight * fields[0][0] + rest * fields[1][0]
-    imag = weight * fields[0][1] + rest * fields[1][1]
+    real = weight * real_ref[0] + rest * real_ref[1]
+    imag = weight * imag_ref[0] + rest * imag_ref[1]
     blend = weight * numbers_ref[2] + rest * numbers_ref[3]
     angle = numbers_ref[1] * numbers_ref[0] * (cell - blend)
     cosine, sine = (jnp.cos(angle), jnp.sin(angle))
@@ -404,8 +431,10 @@
     cells_ref,
     *refs,
 ):
-    *piece_refs, tables_ref, blocks_ref, keep_ref, send_ref = refs
-    result = continued(core_ref[0], numbers_ref, own_ref, other_ref, cells_ref, tables_ref)
+    *piece_refs, tables_ref, blocks_ref, keep_ref, send_ref, real_ref, imag_ref = refs
+    result = continued(
+        core_ref[0], numbers_ref, own_ref, other_ref, cells_ref, tables_ref, real_ref, imag_ref
+    )
     put_blocks(result, blocks_ref)
     above = jnp.concatenate([piece_ref[...] for piece_ref in piece_refs], axis=1)
     values = jnp.where(core_ref[1] == 1, above.reshape(result.shape), result)
@@ -413,9 +442,19 @@
 
 
 def end_kernel(
-    core_ref, numbers_ref, own_ref, other_ref, cells_ref, tables_ref, blocks_ref
+    core_ref,
+    numbers_ref,
+    own_ref,
+    other_ref,
+    cells_ref,
+    tables_ref,
+    blocks_ref,
+    real_ref,
+    imag_ref,
 ):
-    result = continued(core_ref[0], numbers_ref, own_ref, other_ref, cells_ref, tables_ref)
+    result = continued(
+        core_ref[0], numbers_ref, own_ref, other_ref, cells_ref, tables_ref, real_ref, imag_ref
+    )
     put_blocks(result, blocks_ref)
 
 
@@ -443,7 +482,7 @@
             image_ref[lag, :, columns] = total
 
 
-def call(kernel, outs, *args):
+def call(kernel, outs, scratch, *args):
     smem = {0, 1} if kernel_numbers(args) else {0}
     specs = [
         pl.BlockSpec(memory_space=pltpu.SMEM if place in smem else pltpu.VMEM)
@@ -454,6 +493,7 @@
         out_shape=[jax.ShapeDtypeStruct(shape, jnp.float32) for shape in outs],
         in_specs=specs,
         out_specs=[pl.BlockSpec(memory_space=pltpu.VMEM)] * len(outs),
+        scratch_shapes=[pltpu.VMEM(shape, jnp.float32) for shape in scratch],
         compiler_params=pltpu.CompilerParams(vmem_limit_bytes=50 << 20),
         cost_estimate=pl.CostEstimate(
             flops=24 * math.prod(outs[-1]) * args[-1].shape[-1],
@@ -496,7 +536,7 @@
     total_rows = rows * lat
     half_lags = LAGS // 2
     swap = [(d, d + 1 - 2 * (d % 2)) for d in range(depth)]
-    tables = jnp.asarray(dft_tables(width))
+    tables = dft_tables(width)
 
     def halves(value):
         first, second = (value[..., :half], value[..., half:])
@@ -572,7 +612,9 @@
             (lat,) + even.shape
         )
 
-    blocks_one, held = lax.optimization_barrier((cell_blocks(zero, one), held))
+    blocks_one, held, numbers_one, numbers_two = lax.optimization_barrier(
+        (cell_blocks(zero, one), held, numbers_one, numbers_two)
+    )
     cells_one = sent(blocks_one)
     cells_two = lax.ppermute(cells_one, ("depth", "lat"), below_chip)
 
@@ -597,23 +639,39 @@
     middle = functools.partial(middle_kernel, 1.0 / (total_rows * width))
     image_shape = (LAGS, rows, width)
 
-    keep, send = call(start_kernel, spread, core_pair, held, tables)
-    keep, send = call(middle, shifted, core_pair, numbers_one, keep, swapped(send), tables)
+    spectrum = [(total_rows // 2, width)] * 2
+    mixed = [(2, total_rows, half)] * 2
+    keep, send = call(start_kernel, spread, [], core_pair, held, tables)
+    keep, send = call(
+        middle, shifted, spectrum, core_pair, numbers_one, keep, swapped(send), tables
+    )
+    send = swapped(send)
     result, keep, send = call(
         turn_kernel,
         [blocks] + spread,
+        mixed,
         core_pair,
         numbers_one,
         keep,
-        swapped(send),
+        send,
         cells_one,
         *pieces,
         tables,
     )
     first_out = sent(result).reshape((field_count, 2) + blocks[1:])
-    keep, send = call(middle, shifted, core_pair, numbers_two, keep, swapped(send), tables)
+    keep, send = call(
+        middle, shifted, spectrum, core_pair, numbers_two, keep, swapped(send), tables
+    )
     (result,) = call(
-        end_kernel, [blocks], core_pair, numbers_two, keep, swapped(send), cells_two, tables
+        end_kernel,
+        [blocks],
+        mixed,
+        core_pair,
+        numbers_two,
+        keep,
+        swapped(send),
+        cells_two,
+        tables,
     )
     second_out = sent(result).reshape((field_count, 2) + blocks[1:])
 

time: 210 us -> 209 us (level)
  starting transfers between devices: 48.3 us -> 42.7 us
  other arithmetic: 14.8 us -> 17.7 us
    ppermute x1, waiting for transfers between devices: 15.6 us -> 22.8 us  [chip_shards(): cells_two = lax.ppermute(cells_one, ('depth', 'lat'), below_chip)]
    all_to_all x4, waiting for transfers between devices: 53.7 us -> 48.8 us  [sent(): lax.all_to_all(blocks, 'lat', split_axis=0, concat_axis=0, tiled=True)]
    all_to_all x4, starting transfers between devices: 28.9 us -> 24.6 us  [sent(): lax.all_to_all(blocks, 'lat', split_axis=0, concat_axis=0, tiled=True)]
    ppermute x1, waiting for transfers between devices: 3.31 us -> 0.01 us  [chip_shards(): second_numbers = lax.ppermute(first_numbers, ('depth', 'lat'), below_chip)]
  transfers between devices with their start and end apart: 19 -> 19, of which waited for: 10 -> 7; matrix products, arithmetic and copies ran while one was open for 6% -> 8% of each run, Pallas kernels for 17% -> 16%
where the time goes in v2:
time: 209 us; the launch traced here: 208 us
  waiting for transfers between devices  92 us (44%)
  Pallas kernels  49.5 us (24%)
  starting transfers between devices  42.7 us (20%)
  other arithmetic  17.7 us (8%)
  local copies, waits for them, and re-layouts  3.56 us (2%)
  between operations  2.28 us (1%)
    all_to_all x4, waiting for transfers between devices, sent(): lax.all_to_all(blocks, 'lat', split_axis=0, concat_axis=0, tiled=True)  48.8 us
    pallas_call x5, Pallas kernels, call(): pl.pallas_call(kernel, out_shape=[jax.ShapeDtypeStruct(shape, jnp.float32...  45.6 us
    all_to_all x4, starting transfers between devices, sent(): lax.all_to_all(blocks, 'lat', split_axis=0, concat_axis=0, tiled=True)  24.6 us
    ppermute x1, waiting for transfers between devices, chip_shards(): cells_two = lax.ppermute(cells_one, ('depth', 'lat'), below_chip)  22.8 us
    ppermute x1, waiting for transfers between devices, chip_shards(): lax.ppermute(jnp.where(at_first, second_out[:, 0], second_out[:, 1]), 'de...  9.54 us
    ppermute x3, waiting for transfers between devices, chip_shards(): pieces.append(lax.ppermute(surface_part, ('depth', 'lat'), route))  7.59 us
    ppermute x3, starting transfers between devices, chip_shards(): pieces.append(lax.ppermute(surface_part, ('depth', 'lat'), route))  7.25 us
    select_n x1, other arithmetic, chip_shards(): jnp.where(regions[0, 0] == region, region_slowness[0, 0, region], cell)  5.02 us
  transfers between devices with their start and end apart: 19, of which 7 were waited for; matrix products, arithmetic and copies ran while one was open for 8% of the time, Pallas kernels for 16%

profile of v2, /device:TPU:0, one launch (start us, length us, event | category | flops | bytes accessed | tf_op | source)
XLA Modules:
  0.0 207.8 jit_solution(12910064879196735698)
XLA Ops:
  2.5 1.7 slice_select_fusion.2
  7.8 7.1 %all-to-all-start = ((f32[8,80,512]{2,1,0:T(8,128)}), f32[8,80,512]{2,1,0:T(8,128)S(1)}, u32[]{:S(2)}, u32[]{:S(2)}) async-start(f32[8,80,512]{2,1,0:T(8,128)} %pad_maximum_fusion), calls=%async_computation | async-start | bytes 2621440 | tf_op jit(solution)/shard_map/all_to_all | solution.py:549
  14.9 5.0 %select_bitcast_fusion.3 = f32[1,64,512]{2,1,0:T(8,128)S(1)} fusion(s32[1,1,64,512]{3,2,1,0:T(8,128)S(1)} %copy-done.6, f32[]{:T(128)} %bitcast.3, f32[]{:T(128)} %bitcast.4, f32[]{:T(128)} %bitcast.5, f32[]{:T(128)} %bitcast.6, f32[]{:T(128)} %bitcast.7, f32[]{:T(128)} %bitcast.10, f32[]{:T(128)} %bitcast.9, f32[]{:T(128)} %bitcast.8), kind=kLoop, calls=%fused_computation.48 | loop fusion | flops 524288 | bytes 262176 | tf_op jit(solution)/shard_map/jit(_where)/select_n | solution.py:571
  21.0 1.4 maximum_maximum_fusion
  22.5 2.9 %collective-permute-start.3 = (f32[4]{0:T(128)S(1)}, f32[4]{0:T(128)S(1)}, u32[]{:S(2)}, u32[]{:S(2)}) collective-permute-start(f32[4]{0:T(128)S(1)} %broadcast_select_fusion.5), channel_id=1, source_target_pairs={{0,17},{1,0},{2,19},{3,2},{4,21},{5,4},{6,23},{7,6},{8,25},{9,8},{... | collective-permute-start | bytes 56 | tf_op jit(solution)/shard_map/ppermute | solution.py:586
  28.1 18.7 %all-to-all-done.blocks_ref = f32[8,80,512]{2,1,0:T(8,128)S(1)} async-done(((f32[8,80,512]{2,1,0:T(8,128)}), f32[8,80,512]{2,1,0:T(8,128)S(1)}, u32[]{:S(2)}, u32[]{:S(2)}) %all-to-all-start) | async-done | bytes 1310752 | tf_op jit(solution)/shard_map/all_to_all | solution.py:549
  47.9 3.4 %shard_map.113 = (f32[256,512]{1,0:T(8,128)S(1)}, f32[256,512]{1,0:T(8,128)S(1)}) custom-call(s32[2]{0:T(128)S(1)} %pad_add_fusion.core_ref, f32[8,80,512]{2,1,0:T(8,128)S(1)} %all-to-all-done.blocks_ref, bf16[4,512,512]{2,1,0:T(8,128)(2,1)} %bitcast.105), custom_call_target="tpu_custom_call" | custom-call | flops 1610612736 | bytes 1048576 | tf_op jit(solution)/shard_map/pallas_call | solution.py:491
  51.4 4.3 %all-to-all-start.1 = ((f32[8,2,64,256]{3,2,1,0:T(8,128)}), f32[8,2,64,256]{3,2,1,0:T(8,128)}, u32[]{:S(2)}, u32[]{:S(2)}) async-start(f32[8,2,64,256]{3,2,1,0:T(8,128)} %bitcast.110), calls=%async_computation.1 | async-start | bytes 2097152 | tf_op jit(solution)/shard_map/all_to_all | solution.py:549
  56.7 11.4 %shard_map.114 = (f32[2,256,512]{2,1,0:T(8,128)S(1)}, f32[2,256,512]{2,1,0:T(8,128)S(1)}) custom-call(s32[2]{0:T(128)S(1)} %pad_add_fusion.core_ref, f32[4]{0:T(128)S(1)} %pad_maximum_fusion.10.numbers_ref, f32[256,512]{1,0:T(8,128)S(1)} %copy-done.1, f32[256,512]{1,0:T(8,128)S(1)} %collective-permute-done.4.other_ref, bf16[4,512,512]{2,1,0:T(8,128)(2,1)} %bitcast.106), custom_call_target="tpu_custom_call" | custom-call | flops 3221225472 | bytes 2097152 | tf_op jit(solution)/shard_map/pallas_call | solution.py:491
  70.1 5.9 %collective-permute-start.6 = (f32[8,16,512]{2,1,0:T(8,128)S(1)}, f32[8,16,512]{2,1,0:T(8,128)S(1)}, u32[]{:S(2)}, u32[]{:S(2)}) collective-permute-start(f32[8,16,512]{2,1,0:T(8,128)S(1)} %slice.127.refs_3_), channel_id=1, source_target_pairs={{0,17},{2,19},{4,21},{6,23},{8,25},{10,27},{12,29},{14,31}} | collective-permute-start | bytes 786440 | tf_op jit(solution)/shard_map/ppermute | solution.py:634
  76.0 7.6 %collective-permute-done.6.refs_0_ = f32[8,16,512]{2,1,0:T(8,128)S(1)} collective-permute-done((f32[8,16,512]{2,1,0:T(8,128)S(1)}, f32[8,16,512]{2,1,0:T(8,128)S(1)}, u32[]{:S(2)}, u32[]{:S(2)}) %collective-permute-start.6) | collective-permute-done | bytes 262176 | tf_op jit(solution)/shard_map/ppermute | solution.py:634
  83.6 10.9 %shard_map.115 = (f32[8,80,512]{2,1,0:T(8,128)}, f32[256,512]{1,0:T(8,128)S(1)}, f32[256,512]{1,0:T(8,128)S(1)}) custom-call(s32[2]{0:T(128)S(1)} %pad_add_fusion.core_ref, f32[4]{0:T(128)S(1)} %pad_maximum_fusion.10.numbers_ref, f32[2,256,512]{2,1,0:T(8,128)S(1)} %get-tuple-element.20.own_ref, f32[2,256,512]{2,1,0:T(8,128)} %collective-permute-done.5.other_ref, ...), custom_call_target="tpu_custom_call" | custom-call | flops 1610612736 | bytes 2359296 | tf_op jit(solution)/shard_map/pallas_call | solution.py:491
  94.5 7.1 %all-to-all-start.3 = ((f32[8,80,512]{2,1,0:T(8,128)}), f32[8,80,512]{2,1,0:T(8,128)}, u32[]{:S(2)}, u32[]{:S(2)}) async-start(f32[8,80,512]{2,1,0:T(8,128)} %get-tuple-element.27), calls=%async_computation.3 | async-start | bytes 2621440 | tf_op jit(solution)/shard_map/all_to_all | solution.py:549
  101.6 3.9 %collective-permute-start.11 = (f32[8,2,64,256]{3,2,1,0:T(8,128)}, f32[8,2,64,256]{3,2,1,0:T(8,128)S(1)}, u32[]{:S(2)}, u32[]{:S(2)}) collective-permute-start(f32[8,2,64,256]{3,2,1,0:T(8,128)} %all-to-all-done.1.cells_ref), channel_id=1, source_target_pairs={{0,17},{1,0},{2,19},{3,2},{4,21},{5,4},{6,23},{7,6},{8,25},{9,8},{... | collective-permute-start | bytes 3145736 | tf_op jit(solution)/shard_map/ppermute | solution.py:619
  105.6 11.4 %shard_map.116 = (f32[2,256,512]{2,1,0:T(8,128)S(1)}, f32[2,256,512]{2,1,0:T(8,128)S(1)}) custom-call(s32[2]{0:T(128)S(1)} %pad_add_fusion.core_ref, f32[4]{0:T(128)S(1)} %pad_maximum_fusion.11.numbers_ref, f32[256,512]{1,0:T(8,128)S(1)} %get-tuple-element.23.own_ref, f32[256,512]{1,0:T(8,128)S(1)} %collective-permute-done.9.other_ref, ...), custom_call_target="tpu_custom_call" | custom-call | flops 3221225472 | bytes 2097152 | tf_op jit(solution)/shard_map/pallas_call | solution.py:491
  117.3 22.8 %collective-permute-done.11.cells_ref = f32[8,2,64,256]{3,2,1,0:T(8,128)S(1)} collective-permute-done((f32[8,2,64,256]{3,2,1,0:T(8,128)}, f32[8,2,64,256]{3,2,1,0:T(8,128)S(1)}, u32[]{:S(2)}, u32[]{:S(2)}) %collective-permute-start.11) | collective-permute-done | bytes 1048608 | tf_op jit(solution)/shard_map/ppermute | solution.py:619
  140.1 8.5 %shard_map.117 = f32[8,80,512]{2,1,0:T(8,128)} custom-call(s32[2]{0:T(128)S(1)} %pad_add_fusion.core_ref, f32[4]{0:T(128)S(1)} %pad_maximum_fusion.11.numbers_ref, f32[2,256,512]{2,1,0:T(8,128)S(1)} %get-tuple-element.25.own_ref, f32[2,256,512]{2,1,0:T(8,128)S(1)} %collective-permute-done.10.other_ref, ...), custom_call_target="tpu_custom_call" | custom-call | flops 4026531840 | bytes 1310720 | tf_op jit(solution)/shard_map/pallas_call | solution.py:491
  148.6 6.2 %all-to-all-start.2 = ((f32[8,80,512]{2,1,0:T(8,128)}), f32[8,80,512]{2,1,0:T(8,128)S(1)}, u32[]{:S(2)}, u32[]{:S(2)}) async-start(f32[8,80,512]{2,1,0:T(8,128)} %shard_map.117), calls=%async_computation.2 | async-start | bytes 2621440 | tf_op jit(solution)/shard_map/all_to_all | solution.py:549
  156.3 30.1 %all-to-all-done.2 = f32[8,80,512]{2,1,0:T(8,128)S(1)} async-done(((f32[8,80,512]{2,1,0:T(8,128)}), f32[8,80,512]{2,1,0:T(8,128)S(1)}, u32[]{:S(2)}, u32[]{:S(2)}) %all-to-all-start.2) | async-done | bytes 1310752 | tf_op jit(solution)/shard_map/all_to_all | solution.py:549
  186.6 2.2 %collective-permute-start.12 = (f32[4,80,512]{2,1,0:T(8,128)S(1)}, f32[4,80,512]{2,1,0:T(8,128)S(1)}, u32[]{:S(2)}, u32[]{:S(2)}) collective-permute-start(f32[4,80,512]{2,1,0:T(8,128)S(1)} %slice_bitcast_fusion.3), channel_id=1, source_target_pairs={{0,16},{16,0},{1,17},{17,1},{2,18},{18,2},{3,19},{19,3},{4,20},{20... | collective-permute-start | bytes 1966088 | tf_op jit(solution)/shard_map/ppermute | solution.py:692
  188.8 1.5 bitcast_select_fusion
  191.6 9.5 %collective-permute-done.13 = f32[4,80,512]{2,1,0:T(8,128)S(1)} collective-permute-done((f32[4,80,512]{2,1,0:T(8,128)S(1)}, f32[4,80,512]{2,1,0:T(8,128)S(1)}, u32[]{:S(2)}, u32[]{:S(2)}) %collective-permute-start.13) | collective-permute-done | bytes 655392 | tf_op jit(solution)/shard_map/ppermute | solution.py:687
  201.1 2.5 %collective-permute-done.12 = f32[4,80,512]{2,1,0:T(8,128)S(1)} collective-permute-done((f32[4,80,512]{2,1,0:T(8,128)S(1)}, f32[4,80,512]{2,1,0:T(8,128)S(1)}, u32[]{:S(2)}, u32[]{:S(2)}) %collective-permute-start.12) | collective-permute-done | bytes 655392 | tf_op jit(solution)/shard_map/ppermute | solution.py:692
  203.9 2.7 %shard_map.119 = f32[16,64,512]{2,1,0:T(8,128)} custom-call(f32[4,80,512]{2,1,0:T(8,128)S(1)} %get-tuple-element.38.first_ref, f32[4,80,512]{2,1,0:T(8,128)S(1)} %get-tuple-element.39.second_ref, f32[16,64,512]{2,1,0:T(8,128)S(1)} %shard_map.118.refs_0_), custom_call_target="tpu_custom_call" | custom-call | tf_op jit(solution)/shard_map/pallas_call | solution.py:512
  (80 shorter events, 16.7 us)
Async XLA Ops:
  2.0 20.4 %collective-permute-start.2 = (f32[4]{0:T(128)S(1)}, f32[4]{0:T(128)S(1)}, u32[]{:S(2)}, u32[]{:S(2)}) collective-permute-start(f32[4]{0:T(128)S(1)} %pad_maximum_fusion.9), channel_id=1, source_target_pairs={{0,8},{8,0},{16,24},{24,16},{1,9},{9,1},{17,25},{25,17},{2,10},{10... | collective-permute-start | bytes 56 | tf_op jit(solution)/shard_map/ppermute | solution.py:546
  4.3 2.0 collective-permute-start.1
  6.6 8.3 %copy-start.6 = (s32[1,1,64,512]{3,2,1,0:T(8,128)S(1)}, s32[1,1,64,512]{3,2,1,0:T(8,128)}, u32[]{:S(2)}) copy-start(s32[1,1,64,512]{3,2,1,0:T(8,128)} %param.16) | copy-start | bytes 393220
  7.8 12.1 %copy-start.2 = (f32[1,1,64,512]{3,2,1,0:T(8,128)S(1)}, f32[1,1,64,512]{3,2,1,0:T(8,128)}, u32[]{:S(2)}) copy-start(f32[1,1,64,512]{3,2,1,0:T(8,128)} %param.15) | copy-start | bytes 393220
  7.8 12.4 %copy-start.9 = (s32[2]{0:T(128)S(1)}, s32[2]{0:T(128)}, u32[]{:S(2)}) copy-start(s32[2]{0:T(128)} %param.13) | copy-start | bytes 28
  7.8 13.0 %copy-start.4 = (bf16[2,128,512]{2,1,0:T(8,128)(2,1)S(1)}, bf16[2,128,512]{2,1,0:T(8,128)(2,1)}, u32[]{:S(2)}) copy-start(bf16[2,128,512]{2,1,0:T(8,128)(2,1)} %constant.108.clone) | copy-start | bytes 786436
  7.8 13.0 %copy-start.5 = (bf16[2,128,512]{2,1,0:T(8,128)(2,1)S(1)}, bf16[2,128,512]{2,1,0:T(8,128)(2,1)}, u32[]{:S(2)}) copy-start(bf16[2,128,512]{2,1,0:T(8,128)(2,1)} %constant.107.clone) | copy-start | bytes 786436
  7.8 39.0 %all-to-all-start = ((f32[8,80,512]{2,1,0:T(8,128)}), f32[8,80,512]{2,1,0:T(8,128)S(1)}, u32[]{:S(2)}, u32[]{:S(2)}) async-start(f32[8,80,512]{2,1,0:T(8,128)} %pad_maximum_fusion), calls=%async_computation | async-start | bytes 2621440 | tf_op jit(solution)/shard_map/all_to_all | solution.py:549
  20.0 8.1 %collective-permute-start = (f32[2,64,256]{2,1,0:T(8,128)S(1)}, f32[2,64,256]{2,1,0:T(8,128)S(1)}, u32[]{:S(2)}, u32[]{:S(2)}) collective-permute-start(f32[2,64,256]{2,1,0:T(8,128)S(1)} %broadcast_select_fusion.1), channel_id=1, source_target_pairs={{0,8},{8,0},{16,24},{24,16},{1,9},{9,1},{17,25},{25,17},{2,10},{10... | collective-permute-start | bytes 393224 | tf_op jit(solution)/shard_map/ppermute | solution.py:546
  22.5 5.5 %collective-permute-start.3 = (f32[4]{0:T(128)S(1)}, f32[4]{0:T(128)S(1)}, u32[]{:S(2)}, u32[]{:S(2)}) collective-permute-start(f32[4]{0:T(128)S(1)} %broadcast_select_fusion.5), channel_id=1, source_target_pairs={{0,17},{1,0},{2,19},{3,2},{4,21},{5,4},{6,23},{7,6},{8,25},{9,8},{... | collective-permute-start | bytes 56 | tf_op jit(solution)/shard_map/ppermute | solution.py:586
  51.3 4.3 %collective-permute-start.4 = (f32[256,512]{1,0:T(8,128)S(1)}, f32[256,512]{1,0:T(8,128)S(1)}, u32[]{:S(2)}, u32[]{:S(2)}) collective-permute-start(f32[256,512]{1,0:T(8,128)S(1)} %get-tuple-element.19), channel_id=1, source_target_pairs={{0,8},{8,0},{16,24},{24,16},{1,9},{9,1},{17,25},{25,17},{2,10},{10... | collective-permute-start | bytes 1572872 | tf_op jit(solution)/shard_map/ppermute | solution.py:546
  51.4 32.2 %all-to-all-start.1 = ((f32[8,2,64,256]{3,2,1,0:T(8,128)}), f32[8,2,64,256]{3,2,1,0:T(8,128)}, u32[]{:S(2)}, u32[]{:S(2)}) async-start(f32[8,2,64,256]{3,2,1,0:T(8,128)} %bitcast.110), calls=%async_computation.1 | async-start | bytes 2097152 | tf_op jit(solution)/shard_map/all_to_all | solution.py:549
  68.1 15.4 %collective-permute-start.5 = (f32[2,256,512]{2,1,0:T(8,128)S(1)}, f32[2,256,512]{2,1,0:T(8,128)}, u32[]{:S(2)}, u32[]{:S(2)}) collective-permute-start(f32[2,256,512]{2,1,0:T(8,128)S(1)} %get-tuple-element.21), channel_id=1, source_target_pairs={{0,8},{8,0},{16,24},{24,16},{1,9},{9,1},{17,25},{25,17},{2,10},{10... | collective-permute-start | bytes 3145736 | tf_op jit(solution)/shard_map/ppermute | solution.py:546
  68.7 7.3 %collective-permute-start.8 = (f32[8,16,512]{2,1,0:T(8,128)S(1)}, f32[8,16,512]{2,1,0:T(8,128)S(1)}, u32[]{:S(2)}, u32[]{:S(2)}) collective-permute-start(f32[8,16,512]{2,1,0:T(8,128)S(1)} %slice.127.refs_3_), channel_id=1, source_target_pairs={{16,17},{18,19},{20,21},{22,23},{24,25},{26,27},{28,29},{30,31}} | collective-permute-start | bytes 786440 | tf_op jit(solution)/shard_map/ppermute | solution.py:634
  69.4 6.6 %collective-permute-start.7 = (f32[8,16,512]{2,1,0:T(8,128)S(1)}, f32[8,16,512]{2,1,0:T(8,128)S(1)}, u32[]{:S(2)}, u32[]{:S(2)}) collective-permute-start(f32[8,16,512]{2,1,0:T(8,128)S(1)} %slice.127.refs_3_), channel_id=1, source_target_pairs={{1,17},{3,19},{5,21},{7,23},{9,25},{11,27},{13,29},{15,31}} | collective-permute-start | bytes 786440 | tf_op jit(solution)/shard_map/ppermute | solution.py:634
  70.1 13.5 %collective-permute-start.6 = (f32[8,16,512]{2,1,0:T(8,128)S(1)}, f32[8,16,512]{2,1,0:T(8,128)S(1)}, u32[]{:S(2)}, u32[]{:S(2)}) collective-permute-start(f32[8,16,512]{2,1,0:T(8,128)S(1)} %slice.127.refs_3_), channel_id=1, source_target_pairs={{0,17},{2,19},{4,21},{6,23},{8,25},{10,27},{12,29},{14,31}} | collective-permute-start | bytes 786440 | tf_op jit(solution)/shard_map/ppermute | solution.py:634
  94.5 54.1 %all-to-all-start.3 = ((f32[8,80,512]{2,1,0:T(8,128)}), f32[8,80,512]{2,1,0:T(8,128)}, u32[]{:S(2)}, u32[]{:S(2)}) async-start(f32[8,80,512]{2,1,0:T(8,128)} %get-tuple-element.27), calls=%async_computation.3 | async-start | bytes 2621440 | tf_op jit(solution)/shard_map/all_to_all | solution.py:549
  101.6 3.9 %collective-permute-start.9 = (f32[256,512]{1,0:T(8,128)S(1)}, f32[256,512]{1,0:T(8,128)S(1)}, u32[]{:S(2)}, u32[]{:S(2)}) collective-permute-start(f32[256,512]{1,0:T(8,128)S(1)} %get-tuple-element.24), channel_id=1, source_target_pairs={{0,8},{8,0},{16,24},{24,16},{1,9},{9,1},{17,25},{25,17},{2,10},{10... | collective-permute-start | bytes 1572872 | tf_op jit(solution)/shard_map/ppermute | solution.py:546
  101.6 38.5 %collective-permute-start.11 = (f32[8,2,64,256]{3,2,1,0:T(8,128)}, f32[8,2,64,256]{3,2,1,0:T(8,128)S(1)}, u32[]{:S(2)}, u32[]{:S(2)}) collective-permute-start(f32[8,2,64,256]{3,2,1,0:T(8,128)} %all-to-all-done.1.cells_ref), channel_id=1, source_target_pairs={{0,17},{1,0},{2,19},{3,2},{4,21},{5,4},{6,23},{7,6},{8,25},{9,8},{... | collective-permute-start | bytes 3145736 | tf_op jit(solution)/shard_map/ppermute | solution.py:619
  117.0 23.1 %collective-permute-start.10 = (f32[2,256,512]{2,1,0:T(8,128)S(1)}, f32[2,256,512]{2,1,0:T(8,128)S(1)}, u32[]{:S(2)}, u32[]{:S(2)}) collective-permute-start(f32[2,256,512]{2,1,0:T(8,128)S(1)} %get-tuple-element.26), channel_id=1, source_target_pairs={{0,8},{8,0},{16,24},{24,16},{1,9},{9,1},{17,25},{25,17},{2,10},{10... | collective-permute-start | bytes 3145736 | tf_op jit(solution)/shard_map/ppermute | solution.py:546
  148.6 37.7 %all-to-all-start.2 = ((f32[8,80,512]{2,1,0:T(8,128)}), f32[8,80,512]{2,1,0:T(8,128)S(1)}, u32[]{:S(2)}, u32[]{:S(2)}) async-start(f32[8,80,512]{2,1,0:T(8,128)} %shard_map.117), calls=%async_computation.2 | async-start | bytes 2621440 | tf_op jit(solution)/shard_map/all_to_all | solution.py:549
  156.2 32.6 %collective-permute-start.14 = (f32[4,80,512]{2,1,0:T(8,128)S(1)}, f32[4,80,512]{2,1,0:T(8,128)S(1)}, u32[]{:S(2)}, u32[]{:S(2)}) collective-permute-start(f32[4,80,512]{2,1,0:T(8,128)S(1)} %select_bitcast_fusion), channel_id=1, source_target_pairs={{0,8},{8,0},{16,24},{24,16},{1,9},{9,1},{17,25},{25,17},{2,10},{10... | collective-permute-start | bytes 1966088 | tf_op jit(solution)/shard_map/ppermute | solution.py:546
  186.5 14.6 %collective-permute-start.13 = (f32[4,80,512]{2,1,0:T(8,128)S(1)}, f32[4,80,512]{2,1,0:T(8,128)S(1)}, u32[]{:S(2)}, u32[]{:S(2)}) collective-permute-start(f32[4,80,512]{2,1,0:T(8,128)S(1)} %fusion.1), channel_id=1, source_target_pairs={{0,8},{8,16},{16,24},{24,0},{1,9},{9,17},{17,25},{25,1},{2,10},{10... | collective-permute-start | bytes 1966088 | tf_op jit(solution)/shard_map/ppermute | solution.py:687
  186.6 17.0 %collective-permute-start.12 = (f32[4,80,512]{2,1,0:T(8,128)S(1)}, f32[4,80,512]{2,1,0:T(8,128)S(1)}, u32[]{:S(2)}, u32[]{:S(2)}) collective-permute-start(f32[4,80,512]{2,1,0:T(8,128)S(1)} %slice_bitcast_fusion.3), channel_id=1, source_target_pairs={{0,16},{16,0},{1,17},{17,1},{2,18},{18,2},{3,19},{19,3},{4,20},{20... | collective-permute-start | bytes 1966088 | tf_op jit(solution)/shard_map/ppermute | solution.py:692
  (5 other events, 13.6 us)

commit v3 on v2

--- a/solution.py
+++ b/solution.py
@@ -330,6 +330,21 @@
     spread_rows(core_ref[0], tables_ref, values, keep_ref, send_ref)
 
 
+def series(square, first):
+    total = jnp.ones_like(square)
+    for step in range(first + 14, first, -2):
+        total = 1.0 - square * (total * (1.0 / (step * (step - 1))))
+    return total
+
+
+def cos_sin(angle):
+    quarter = 0.5 * angle
+    square = quarter * quarter
+    sine = quarter * series(square, 1)
+    cosine = series(square, 0)
+    return (1.0 - 2.0 * (sine * sine), 2.0 * (sine * cosine))
+
+
 def folded(positions, length):
     moved = jnp.where(positions < length // 2, positions, positions - length)
     return moved.astype(jnp.float32) * (2.0 * math.pi / length)
@@ -374,8 +389,9 @@
         gap = base * base - squared
         amplitude = jnp.exp(-jnp.sqrt(jnp.maximum(-gap, 0.0))) * scale
         turning = jnp.sqrt(jnp.maximum(gap, 0.0))
-        cosine = amplitude * jnp.cos(turning)
-        sine = amplitude * (sign * jnp.sin(turning))
+        cosine, sine = cos_sin(turning)
+        cosine = amplitude * cosine
+        sine = amplitude * (sign * sine)
         shifted = jnp.concatenate([real * cosine - imag * sine, real * sine + imag * cosine], axis=0)
         back_real, back_imag = dft_right(tables_ref, shifted, 1.0)
         first = jnp.concatenate([back_real[:, :half], back_imag[:, :half]], axis=1)
@@ -404,7 +420,7 @@
     imag = weight * imag_ref[0] + rest * imag_ref[1]
     blend = weight * numbers_ref[2] + rest * numbers_ref[3]
     angle = numbers_ref[1] * numbers_ref[0] * (cell - blend)
-    cosine, sine = (jnp.cos(angle), jnp.sin(angle))
+    cosine, sine = cos_sin(angle)
     return jnp.concatenate([real * cosine - imag * sine, real * sine + imag * cosine], axis=1)
 
 
@@ -642,9 +658,8 @@
     spectrum = [(total_rows // 2, width)] * 2
     mixed = [(2, total_rows, half)] * 2
     keep, send = call(start_kernel, spread, [], core_pair, held, tables)
-    keep, send = call(
-        middle, shifted, spectrum, core_pair, numbers_one, keep, swapped(send), tables
-    )
+    send = swapped(send)
+    keep, send = call(middle, shifted, spectrum, core_pair, numbers_one, keep, send, tables)
     send = swapped(send)
     result, keep, send = call(
         turn_kernel,

time: 209 us -> 205 us (0.981)
  Pallas kernels: 49.5 us -> 43.6 us
  waiting for transfers between devices: 92 us -> 94.3 us
    pallas_call x5, Pallas kernels: 45.6 us -> 39.7 us  [call(): pl.pallas_call(kernel, out_shape=[jax.ShapeDtypeStruct(shape, jnp.float32...]
  transfers between devices with their start and end apart: 19 -> 19, of which waited for: 7 -> 8; matrix products, arithmetic and copies ran while one was open for 8% -> 8% of each run, Pallas kernels for 16% -> 14%
where the time goes in v3:
time: 205 us; the launch traced here: 204 us
  waiting for transfers between devices  94.3 us (46%)
  Pallas kernels  43.6 us (21%)
  starting transfers between devices  42.4 us (21%)
  other arithmetic  17.7 us (9%)
  local copies, waits for them, and re-layouts  3.56 us (2%)
  between operations  2.28 us (1%)
    all_to_all x4, waiting for transfers between devices, sent(): lax.all_to_all(blocks, 'lat', split_axis=0, concat_axis=0, tiled=True)  49.5 us
    pallas_call x5, Pallas kernels, call(): pl.pallas_call(kernel, out_shape=[jax.ShapeDtypeStruct(shape, jnp.float32...  39.7 us
    all_to_all x4, starting transfers between devices, sent(): lax.all_to_all(blocks, 'lat', split_axis=0, concat_axis=0, tiled=True)  24.6 us
    ppermute x1, waiting for transfers between devices, chip_shards(): cells_two = lax.ppermute(cells_one, ('depth', 'lat'), below_chip)  24 us
    ppermute x1, waiting for transfers between devices, chip_shards(): lax.ppermute(jnp.where(at_first, second_out[:, 0], second_out[:, 1]), 'de...  9.76 us
    ppermute x3, waiting for transfers between devices, chip_shards(): pieces.append(lax.ppermute(surface_part, ('depth', 'lat'), route))  7.81 us
    ppermute x3, starting transfers between devices, chip_shards(): pieces.append(lax.ppermute(surface_part, ('depth', 'lat'), route))  7.05 us
    select_n x1, other arithmetic, chip_shards(): jnp.where(regions[0, 0] == region, region_slowness[0, 0, region], cell)  5.02 us
  transfers between devices with their start and end apart: 19, of which 8 were waited for; matrix products, arithmetic and copies ran while one was open for 8% of the time, Pallas kernels for 14%

profile of v3, /device:TPU:0, one launch (start us, length us, event | category | flops | bytes accessed | tf_op | source)
XLA Modules:
  0.0 203.8 jit_solution(18356680616978612365)
XLA Ops:
  2.5 1.7 slice_select_fusion.2
  7.8 7.1 %all-to-all-start = ((f32[8,80,512]{2,1,0:T(8,128)}), f32[8,80,512]{2,1,0:T(8,128)S(1)}, u32[]{:S(2)}, u32[]{:S(2)}) async-start(f32[8,80,512]{2,1,0:T(8,128)} %pad_maximum_fusion), calls=%async_computation | async-start | bytes 2621440 | tf_op jit(solution)/shard_map/all_to_all | solution.py:565
  14.9 5.0 %select_bitcast_fusion.3 = f32[1,64,512]{2,1,0:T(8,128)S(1)} fusion(s32[1,1,64,512]{3,2,1,0:T(8,128)S(1)} %copy-done.6, f32[]{:T(128)} %bitcast.3, f32[]{:T(128)} %bitcast.4, f32[]{:T(128)} %bitcast.5, f32[]{:T(128)} %bitcast.6, f32[]{:T(128)} %bitcast.7, f32[]{:T(128)} %bitcast.10, f32[]{:T(128)} %bitcast.9, f32[]{:T(128)} %bitcast.8), kind=kLoop, calls=%fused_computation.48 | loop fusion | flops 524288 | bytes 262176 | tf_op jit(solution)/shard_map/jit(_where)/select_n | solution.py:587
  21.0 1.4 maximum_maximum_fusion
  22.5 2.9 %collective-permute-start.3 = (f32[4]{0:T(128)S(1)}, f32[4]{0:T(128)S(1)}, u32[]{:S(2)}, u32[]{:S(2)}) collective-permute-start(f32[4]{0:T(128)S(1)} %broadcast_select_fusion.5), channel_id=1, source_target_pairs={{0,17},{1,0},{2,19},{3,2},{4,21},{5,4},{6,23},{7,6},{8,25},{9,8},{... | collective-permute-start | bytes 56 | tf_op jit(solution)/shard_map/ppermute | solution.py:602
  28.1 18.7 %all-to-all-done.blocks_ref = f32[8,80,512]{2,1,0:T(8,128)S(1)} async-done(((f32[8,80,512]{2,1,0:T(8,128)}), f32[8,80,512]{2,1,0:T(8,128)S(1)}, u32[]{:S(2)}, u32[]{:S(2)}) %all-to-all-start) | async-done | bytes 1310752 | tf_op jit(solution)/shard_map/all_to_all | solution.py:565
  47.9 3.4 %shard_map.113 = (f32[256,512]{1,0:T(8,128)S(1)}, f32[256,512]{1,0:T(8,128)S(1)}) custom-call(s32[2]{0:T(128)S(1)} %pad_add_fusion.core_ref, f32[8,80,512]{2,1,0:T(8,128)S(1)} %all-to-all-done.blocks_ref, bf16[4,512,512]{2,1,0:T(8,128)(2,1)} %bitcast.105), custom_call_target="tpu_custom_call" | custom-call | flops 1610612736 | bytes 1048576 | tf_op jit(solution)/shard_map/pallas_call | solution.py:507
  51.4 4.3 %all-to-all-start.1 = ((f32[8,2,64,256]{3,2,1,0:T(8,128)}), f32[8,2,64,256]{3,2,1,0:T(8,128)}, u32[]{:S(2)}, u32[]{:S(2)}) async-start(f32[8,2,64,256]{3,2,1,0:T(8,128)} %bitcast.110), calls=%async_computation.1 | async-start | bytes 2097152 | tf_op jit(solution)/shard_map/all_to_all | solution.py:565
  56.7 9.4 %shard_map.114 = (f32[2,256,512]{2,1,0:T(8,128)S(1)}, f32[2,256,512]{2,1,0:T(8,128)S(1)}) custom-call(s32[2]{0:T(128)S(1)} %pad_add_fusion.core_ref, f32[4]{0:T(128)S(1)} %pad_maximum_fusion.10.numbers_ref, f32[256,512]{1,0:T(8,128)S(1)} %copy-done.1, f32[256,512]{1,0:T(8,128)S(1)} %collective-permute-done.4.other_ref, bf16[4,512,512]{2,1,0:T(8,128)(2,1)} %bitcast.106), custom_call_target="tpu_custom_call" | custom-call | flops 3221225472 | bytes 2097152 | tf_op jit(solution)/shard_map/pallas_call | solution.py:507
  68.1 5.7 %collective-permute-start.6 = (f32[8,16,512]{2,1,0:T(8,128)S(1)}, f32[8,16,512]{2,1,0:T(8,128)S(1)}, u32[]{:S(2)}, u32[]{:S(2)}) collective-permute-start(f32[8,16,512]{2,1,0:T(8,128)S(1)} %slice.127.refs_3_), channel_id=1, source_target_pairs={{0,17},{2,19},{4,21},{6,23},{8,25},{10,27},{12,29},{14,31}} | collective-permute-start | bytes 786440 | tf_op jit(solution)/shard_map/ppermute | solution.py:650
  73.8 7.8 %collective-permute-done.6.refs_0_ = f32[8,16,512]{2,1,0:T(8,128)S(1)} collective-permute-done((f32[8,16,512]{2,1,0:T(8,128)S(1)}, f32[8,16,512]{2,1,0:T(8,128)S(1)}, u32[]{:S(2)}, u32[]{:S(2)}) %collective-permute-start.6) | collective-permute-done | bytes 262176 | tf_op jit(solution)/shard_map/ppermute | solution.py:650
  82.4 9.9 %shard_map.115 = (f32[8,80,512]{2,1,0:T(8,128)}, f32[256,512]{1,0:T(8,128)S(1)}, f32[256,512]{1,0:T(8,128)S(1)}) custom-call(s32[2]{0:T(128)S(1)} %pad_add_fusion.core_ref, f32[4]{0:T(128)S(1)} %pad_maximum_fusion.10.numbers_ref, f32[2,256,512]{2,1,0:T(8,128)S(1)} %get-tuple-element.20.own_ref, f32[2,256,512]{2,1,0:T(8,128)} %collective-permute-done.5.other_ref, ...), custom_call_target="tpu_custom_call" | custom-call | flops 1610612736 | bytes 2359296 | tf_op jit(solution)/shard_map/pallas_call | solution.py:507
  92.3 6.3 %all-to-all-start.3 = ((f32[8,80,512]{2,1,0:T(8,128)}), f32[8,80,512]{2,1,0:T(8,128)}, u32[]{:S(2)}, u32[]{:S(2)}) async-start(f32[8,80,512]{2,1,0:T(8,128)} %get-tuple-element.27), calls=%async_computation.3 | async-start | bytes 2621440 | tf_op jit(solution)/shard_map/all_to_all | solution.py:565
  98.7 3.9 %collective-permute-start.11 = (f32[8,2,64,256]{3,2,1,0:T(8,128)}, f32[8,2,64,256]{3,2,1,0:T(8,128)S(1)}, u32[]{:S(2)}, u32[]{:S(2)}) collective-permute-start(f32[8,2,64,256]{3,2,1,0:T(8,128)} %all-to-all-done.1.cells_ref), channel_id=1, source_target_pairs={{0,17},{1,0},{2,19},{3,2},{4,21},{5,4},{6,23},{7,6},{8,25},{9,8},{... | collective-permute-start | bytes 3145736 | tf_op jit(solution)/shard_map/ppermute | solution.py:635
  102.6 9.4 %shard_map.116 = (f32[2,256,512]{2,1,0:T(8,128)S(1)}, f32[2,256,512]{2,1,0:T(8,128)S(1)}) custom-call(s32[2]{0:T(128)S(1)} %pad_add_fusion.core_ref, f32[4]{0:T(128)S(1)} %pad_maximum_fusion.11.numbers_ref, f32[256,512]{1,0:T(8,128)S(1)} %get-tuple-element.23.own_ref, f32[256,512]{1,0:T(8,128)S(1)} %collective-permute-done.9.other_ref, ...), custom_call_target="tpu_custom_call" | custom-call | flops 3221225472 | bytes 2097152 | tf_op jit(solution)/shard_map/pallas_call | solution.py:507
  112.3 24.0 %collective-permute-done.11.cells_ref = f32[8,2,64,256]{3,2,1,0:T(8,128)S(1)} collective-permute-done((f32[8,2,64,256]{3,2,1,0:T(8,128)}, f32[8,2,64,256]{3,2,1,0:T(8,128)S(1)}, u32[]{:S(2)}, u32[]{:S(2)}) %collective-permute-start.11) | collective-permute-done | bytes 1048608 | tf_op jit(solution)/shard_map/ppermute | solution.py:635
  136.4 7.5 %shard_map.117 = f32[8,80,512]{2,1,0:T(8,128)} custom-call(s32[2]{0:T(128)S(1)} %pad_add_fusion.core_ref, f32[4]{0:T(128)S(1)} %pad_maximum_fusion.11.numbers_ref, f32[2,256,512]{2,1,0:T(8,128)S(1)} %get-tuple-element.25.own_ref, f32[2,256,512]{2,1,0:T(8,128)S(1)} %collective-permute-done.10.other_ref, ...), custom_call_target="tpu_custom_call" | custom-call | flops 4026531840 | bytes 1310720 | tf_op jit(solution)/shard_map/pallas_call | solution.py:507
  143.9 6.9 %all-to-all-start.2 = ((f32[8,80,512]{2,1,0:T(8,128)}), f32[8,80,512]{2,1,0:T(8,128)S(1)}, u32[]{:S(2)}, u32[]{:S(2)}) async-start(f32[8,80,512]{2,1,0:T(8,128)} %shard_map.117), calls=%async_computation.2 | async-start | bytes 2621440 | tf_op jit(solution)/shard_map/all_to_all | solution.py:565
  152.3 30.1 %all-to-all-done.2 = f32[8,80,512]{2,1,0:T(8,128)S(1)} async-done(((f32[8,80,512]{2,1,0:T(8,128)}), f32[8,80,512]{2,1,0:T(8,128)S(1)}, u32[]{:S(2)}, u32[]{:S(2)}) %all-to-all-start.2) | async-done | bytes 1310752 | tf_op jit(solution)/shard_map/all_to_all | solution.py:565
  182.6 2.0 collective-permute-start.12
  184.7 1.5 bitcast_select_fusion
  187.4 9.8 %collective-permute-done.13 = f32[4,80,512]{2,1,0:T(8,128)S(1)} collective-permute-done((f32[4,80,512]{2,1,0:T(8,128)S(1)}, f32[4,80,512]{2,1,0:T(8,128)S(1)}, u32[]{:S(2)}, u32[]{:S(2)}) %collective-permute-start.13) | collective-permute-done | bytes 655392 | tf_op jit(solution)/shard_map/ppermute | solution.py:702
  197.2 2.5 %collective-permute-done.12 = f32[4,80,512]{2,1,0:T(8,128)S(1)} collective-permute-done((f32[4,80,512]{2,1,0:T(8,128)S(1)}, f32[4,80,512]{2,1,0:T(8,128)S(1)}, u32[]{:S(2)}, u32[]{:S(2)}) %collective-permute-start.12) | collective-permute-done | bytes 655392 | tf_op jit(solution)/shard_map/ppermute | solution.py:707
  199.9 2.7 %shard_map.119 = f32[16,64,512]{2,1,0:T(8,128)} custom-call(f32[4,80,512]{2,1,0:T(8,128)S(1)} %get-tuple-element.38.first_ref, f32[4,80,512]{2,1,0:T(8,128)S(1)} %get-tuple-element.39.second_ref, f32[16,64,512]{2,1,0:T(8,128)S(1)} %shard_map.118.refs_0_), custom_call_target="tpu_custom_call" | custom-call | tf_op jit(solution)/shard_map/pallas_call | solution.py:528
  (80 shorter events, 17.5 us)
Async XLA Ops:
  2.0 20.4 %collective-permute-start.2 = (f32[4]{0:T(128)S(1)}, f32[4]{0:T(128)S(1)}, u32[]{:S(2)}, u32[]{:S(2)}) collective-permute-start(f32[4]{0:T(128)S(1)} %pad_maximum_fusion.9), channel_id=1, source_target_pairs={{0,8},{8,0},{16,24},{24,16},{1,9},{9,1},{17,25},{25,17},{2,10},{10... | collective-permute-start | bytes 56 | tf_op jit(solution)/shard_map/ppermute | solution.py:562
  4.3 2.0 collective-permute-start.1
  6.6 8.3 %copy-start.6 = (s32[1,1,64,512]{3,2,1,0:T(8,128)S(1)}, s32[1,1,64,512]{3,2,1,0:T(8,128)}, u32[]{:S(2)}) copy-start(s32[1,1,64,512]{3,2,1,0:T(8,128)} %param.16) | copy-start | bytes 393220
  7.8 12.1 %copy-start.2 = (f32[1,1,64,512]{3,2,1,0:T(8,128)S(1)}, f32[1,1,64,512]{3,2,1,0:T(8,128)}, u32[]{:S(2)}) copy-start(f32[1,1,64,512]{3,2,1,0:T(8,128)} %param.15) | copy-start | bytes 393220
  7.8 12.4 %copy-start.9 = (s32[2]{0:T(128)S(1)}, s32[2]{0:T(128)}, u32[]{:S(2)}) copy-start(s32[2]{0:T(128)} %param.13) | copy-start | bytes 28
  7.8 13.0 %copy-start.4 = (bf16[2,128,512]{2,1,0:T(8,128)(2,1)S(1)}, bf16[2,128,512]{2,1,0:T(8,128)(2,1)}, u32[]{:S(2)}) copy-start(bf16[2,128,512]{2,1,0:T(8,128)(2,1)} %constant.108.clone) | copy-start | bytes 786436
  7.8 13.0 %copy-start.5 = (bf16[2,128,512]{2,1,0:T(8,128)(2,1)S(1)}, bf16[2,128,512]{2,1,0:T(8,128)(2,1)}, u32[]{:S(2)}) copy-start(bf16[2,128,512]{2,1,0:T(8,128)(2,1)} %constant.107.clone) | copy-start | bytes 786436
  7.8 39.0 %all-to-all-start = ((f32[8,80,512]{2,1,0:T(8,128)}), f32[8,80,512]{2,1,0:T(8,128)S(1)}, u32[]{:S(2)}, u32[]{:S(2)}) async-start(f32[8,80,512]{2,1,0:T(8,128)} %pad_maximum_fusion), calls=%async_computation | async-start | bytes 2621440 | tf_op jit(solution)/shard_map/all_to_all | solution.py:565
  20.0 8.1 %collective-permute-start = (f32[2,64,256]{2,1,0:T(8,128)S(1)}, f32[2,64,256]{2,1,0:T(8,128)S(1)}, u32[]{:S(2)}, u32[]{:S(2)}) collective-permute-start(f32[2,64,256]{2,1,0:T(8,128)S(1)} %broadcast_select_fusion.1), channel_id=1, source_target_pairs={{0,8},{8,0},{16,24},{24,16},{1,9},{9,1},{17,25},{25,17},{2,10},{10... | collective-permute-start | bytes 393224 | tf_op jit(solution)/shard_map/ppermute | solution.py:562
  22.5 5.5 %collective-permute-start.3 = (f32[4]{0:T(128)S(1)}, f32[4]{0:T(128)S(1)}, u32[]{:S(2)}, u32[]{:S(2)}) collective-permute-start(f32[4]{0:T(128)S(1)} %broadcast_select_fusion.5), channel_id=1, source_target_pairs={{0,17},{1,0},{2,19},{3,2},{4,21},{5,4},{6,23},{7,6},{8,25},{9,8},{... | collective-permute-start | bytes 56 | tf_op jit(solution)/shard_map/ppermute | solution.py:602
  51.3 4.3 %collective-permute-start.4 = (f32[256,512]{1,0:T(8,128)S(1)}, f32[256,512]{1,0:T(8,128)S(1)}, u32[]{:S(2)}, u32[]{:S(2)}) collective-permute-start(f32[256,512]{1,0:T(8,128)S(1)} %get-tuple-element.19), channel_id=1, source_target_pairs={{0,8},{8,0},{16,24},{24,16},{1,9},{9,1},{17,25},{25,17},{2,10},{10... | collective-permute-start | bytes 1572872 | tf_op jit(solution)/shard_map/ppermute | solution.py:562
  51.4 31.0 %all-to-all-start.1 = ((f32[8,2,64,256]{3,2,1,0:T(8,128)}), f32[8,2,64,256]{3,2,1,0:T(8,128)}, u32[]{:S(2)}, u32[]{:S(2)}) async-start(f32[8,2,64,256]{3,2,1,0:T(8,128)} %bitcast.110), calls=%async_computation.1 | async-start | bytes 2097152 | tf_op jit(solution)/shard_map/all_to_all | solution.py:565
  66.2 15.5 %collective-permute-start.5 = (f32[2,256,512]{2,1,0:T(8,128)S(1)}, f32[2,256,512]{2,1,0:T(8,128)}, u32[]{:S(2)}, u32[]{:S(2)}) collective-permute-start(f32[2,256,512]{2,1,0:T(8,128)S(1)} %get-tuple-element.21), channel_id=1, source_target_pairs={{0,8},{8,0},{16,24},{24,16},{1,9},{9,1},{17,25},{25,17},{2,10},{10... | collective-permute-start | bytes 3145736 | tf_op jit(solution)/shard_map/ppermute | solution.py:562
  66.7 7.1 %collective-permute-start.8 = (f32[8,16,512]{2,1,0:T(8,128)S(1)}, f32[8,16,512]{2,1,0:T(8,128)S(1)}, u32[]{:S(2)}, u32[]{:S(2)}) collective-permute-start(f32[8,16,512]{2,1,0:T(8,128)S(1)} %slice.127.refs_3_), channel_id=1, source_target_pairs={{16,17},{18,19},{20,21},{22,23},{24,25},{26,27},{28,29},{30,31}} | collective-permute-start | bytes 786440 | tf_op jit(solution)/shard_map/ppermute | solution.py:650
  67.4 6.4 %collective-permute-start.7 = (f32[8,16,512]{2,1,0:T(8,128)S(1)}, f32[8,16,512]{2,1,0:T(8,128)S(1)}, u32[]{:S(2)}, u32[]{:S(2)}) collective-permute-start(f32[8,16,512]{2,1,0:T(8,128)S(1)} %slice.127.refs_3_), channel_id=1, source_target_pairs={{1,17},{3,19},{5,21},{7,23},{9,25},{11,27},{13,29},{15,31}} | collective-permute-start | bytes 786440 | tf_op jit(solution)/shard_map/ppermute | solution.py:650
  68.1 13.5 %collective-permute-start.6 = (f32[8,16,512]{2,1,0:T(8,128)S(1)}, f32[8,16,512]{2,1,0:T(8,128)S(1)}, u32[]{:S(2)}, u32[]{:S(2)}) collective-permute-start(f32[8,16,512]{2,1,0:T(8,128)S(1)} %slice.127.refs_3_), channel_id=1, source_target_pairs={{0,17},{2,19},{4,21},{6,23},{8,25},{10,27},{12,29},{14,31}} | collective-permute-start | bytes 786440 | tf_op jit(solution)/shard_map/ppermute | solution.py:650
  92.3 51.6 %all-to-all-start.3 = ((f32[8,80,512]{2,1,0:T(8,128)}), f32[8,80,512]{2,1,0:T(8,128)}, u32[]{:S(2)}, u32[]{:S(2)}) async-start(f32[8,80,512]{2,1,0:T(8,128)} %get-tuple-element.27), calls=%async_computation.3 | async-start | bytes 2621440 | tf_op jit(solution)/shard_map/all_to_all | solution.py:565
  98.7 3.9 %collective-permute-start.9 = (f32[256,512]{1,0:T(8,128)S(1)}, f32[256,512]{1,0:T(8,128)S(1)}, u32[]{:S(2)}, u32[]{:S(2)}) collective-permute-start(f32[256,512]{1,0:T(8,128)S(1)} %get-tuple-element.24), channel_id=1, source_target_pairs={{0,8},{8,0},{16,24},{24,16},{1,9},{9,1},{17,25},{25,17},{2,10},{10... | collective-permute-start | bytes 1572872 | tf_op jit(solution)/shard_map/ppermute | solution.py:562
  98.7 37.7 %collective-permute-start.11 = (f32[8,2,64,256]{3,2,1,0:T(8,128)}, f32[8,2,64,256]{3,2,1,0:T(8,128)S(1)}, u32[]{:S(2)}, u32[]{:S(2)}) collective-permute-start(f32[8,2,64,256]{3,2,1,0:T(8,128)} %all-to-all-done.1.cells_ref), channel_id=1, source_target_pairs={{0,17},{1,0},{2,19},{3,2},{4,21},{5,4},{6,23},{7,6},{8,25},{9,8},{... | collective-permute-start | bytes 3145736 | tf_op jit(solution)/shard_map/ppermute | solution.py:635
  112.0 24.4 %collective-permute-start.10 = (f32[2,256,512]{2,1,0:T(8,128)S(1)}, f32[2,256,512]{2,1,0:T(8,128)S(1)}, u32[]{:S(2)}, u32[]{:S(2)}) collective-permute-start(f32[2,256,512]{2,1,0:T(8,128)S(1)} %get-tuple-element.26), channel_id=1, source_target_pairs={{0,8},{8,0},{16,24},{24,16},{1,9},{9,1},{17,25},{25,17},{2,10},{10... | collective-permute-start | bytes 3145736 | tf_op jit(solution)/shard_map/ppermute | solution.py:562
  143.9 38.5 %all-to-all-start.2 = ((f32[8,80,512]{2,1,0:T(8,128)}), f32[8,80,512]{2,1,0:T(8,128)S(1)}, u32[]{:S(2)}, u32[]{:S(2)}) async-start(f32[8,80,512]{2,1,0:T(8,128)} %shard_map.117), calls=%async_computation.2 | async-start | bytes 2621440 | tf_op jit(solution)/shard_map/all_to_all | solution.py:565
  152.2 32.4 %collective-permute-start.14 = (f32[4,80,512]{2,1,0:T(8,128)S(1)}, f32[4,80,512]{2,1,0:T(8,128)S(1)}, u32[]{:S(2)}, u32[]{:S(2)}) collective-permute-start(f32[4,80,512]{2,1,0:T(8,128)S(1)} %select_bitcast_fusion), channel_id=1, source_target_pairs={{0,8},{8,0},{16,24},{24,16},{1,9},{9,1},{17,25},{25,17},{2,10},{10... | collective-permute-start | bytes 1966088 | tf_op jit(solution)/shard_map/ppermute | solution.py:562
  182.6 14.6 %collective-permute-start.13 = (f32[4,80,512]{2,1,0:T(8,128)S(1)}, f32[4,80,512]{2,1,0:T(8,128)S(1)}, u32[]{:S(2)}, u32[]{:S(2)}) collective-permute-start(f32[4,80,512]{2,1,0:T(8,128)S(1)} %fusion.1), channel_id=1, source_target_pairs={{0,8},{8,16},{16,24},{24,0},{1,9},{9,17},{17,25},{25,1},{2,10},{10... | collective-permute-start | bytes 1966088 | tf_op jit(solution)/shard_map/ppermute | solution.py:702
  182.6 17.0 %collective-permute-start.12 = (f32[4,80,512]{2,1,0:T(8,128)S(1)}, f32[4,80,512]{2,1,0:T(8,128)S(1)}, u32[]{:S(2)}, u32[]{:S(2)}) collective-permute-start(f32[4,80,512]{2,1,0:T(8,128)S(1)} %slice_bitcast_fusion.3), channel_id=1, source_target_pairs={{0,16},{16,0},{1,17},{17,1},{2,18},{18,2},{3,19},{19,3},{4,20},{20... | collective-permute-start | bytes 1966088 | tf_op jit(solution)/shard_map/ppermute | solution.py:707
  (5 other events, 13.6 us)
